TPU v7x, 128 devices: a whole 4x4x4 slice. The times are simulated.
128 devices in a mesh: slab: 8 (over x, y_hi), plane: 16 (over z, y_lo, core).
Axes of the slice: x: 4, y: 4 (y_hi: 2, y_lo: 2; y = y_hi * 2 + y_lo), z: 4, core: 2. Of those that a mesh axis runs over, the one named last changes fastest.
Arguments:
- images: float32 [2, 64, 256, 1024], P(None, 'slab', 'plane'), may hold values from -12 to 12, as said below
- shifts: int32 [3, 8, 32, 128], P(None, 'slab', 'plane'), may hold values from -1 to 1
- initial_displacement: float32 [3, 8, 32, 128], P(None, 'slab', 'plane'), may hold values from -2 to 2
Outputs:
- displacement: float32 [3, 8, 32, 128], P(None, 'slab', 'plane')
- mismatch: float32 [64, 256, 1024], P('slab', 'plane')
Inputs may be any that keep to these rules, and one draw needn't show every extreme that they name: `images`: voxel intensities.
All inputs are finite; a program needn't handle non-finite values.
Results may differ from a plain program's by a relative error of at most 0.0023.
Values sent between devices are 32-bit elements; how exact they have to be, the bound alone decides.
No kernel may reach another device: no remote copies, remote signals or barrier semaphores. Data moves between devices by JAX's collectives and lax.ppermute only.
A program may use at most 192 MiB of HBM per device.

v0:
```python
import jax
import jax.numpy as jnp
import numpy as np
from jax import lax
from jax.experimental import pallas as pl
from jax.experimental.pallas import tpu as pltpu
from jax.sharding import PartitionSpec as P


ITERS = 6
reg_weight = 4.0
AXES = ("slab", "plane")
NCHUNK = 8
ROWS = 112
RHS_ROW = 96
U_ROW = 102
ENERGY_ROW = 108
COLORS = ((0, 40), (40, 40), (80, 32))
STRIDE = 136
LIMIT_A = 2 << 20
LIMIT_B = 9 << 20
PAIRS = ((0, 0), (0, 1), (0, 2), (1, 1), (1, 2), (2, 2))
AB = [[0, 1, 2], [1, 3, 4], [2, 4, 5]]
F32 = jnp.float32
BF16 = jnp.bfloat16


def build_constants():
    w = np.arange(8) / 8.0
    lo, up = 1.0 - w, w
    quad = (lo * lo, lo * up, up * up)
    lin = (lo, up)
    wq = np.zeros((1024, 256))
    wl = np.zeros((1024, 128))
    for e in range(128):
        for i in range(8):
            v = 8 * e + i
            wq[v, e] += quad[0][i]
            wq[v, 128 + e] += quad[1][i]
            wl[v, e] += lin[0][i]
            if e + 1 < 128:
                wq[v, e + 1] += quad[2][i]
                wl[v, e + 1] += lin[1][i]
    spread = np.zeros((128, 1024))
    for e in range(128):
        spread[e, 8 * e : 8 * e + 8] = 1.0
    ly = np.zeros((4, 48, 288))
    ry = np.zeros((4, 24, 288))

    def put(which, tz, yk, zt, er, yq):
        for ab in range(6):
            for s in range(8):
                ly[which, (tz * 4 + yk) * 6 + ab, ((zt * 6 + ab) * 2 + er) * 8 + s] += quad[yq][s]

    for which, tz, zt in ((0, 0, 0), (0, 1, 1), (1, 0, 2)):
        put(which, tz, 0, zt, 0, 0)
        put(which, tz, 1, zt, 0, 2)
        put(which, tz, 1, zt, 1, 0)
        put(which, tz, 2, zt, 0, 1)
        put(which, tz, 3, zt, 1, 1)
    for which, tz, zt in ((2, 0, 0), (2, 1, 1), (3, 0, 2)):
        put(which, tz, 0, zt, 1, 2)

    def put_rhs(which, yl, zt, er, yq):
        for c in range(9):
            for s in range(8):
                ry[which, yl * 9 + c, ((zt * 9 + c) * 2 + er) * 8 + s] += lin[yq][s]

    for which, zt in ((0, 0), (1, 1)):
        put_rhs(which, 0, zt, 0, 0)
        put_rhs(which, 1, zt, 0, 1)
        put_rhs(which, 1, zt, 1, 0)
    for which, zt in ((2, 0), (3, 1)):
        put_rhs(which, 0, zt, 1, 1)
    cast = lambda a: jnp.asarray(a.astype(np.float32)).astype(BF16)
    return (
        cast(np.concatenate([wq, wl], 1)),
        cast(np.concatenate([wl.T, spread], 0)),
        cast(np.concatenate([ly.reshape(192, 288), ry.reshape(96, 288)], 0)),
    )


def dot(a, b):
    return lax.dot_general(a, b, (((1,), (0,)), ((), ())), preferred_element_type=F32)


def split_left(a, b, parts=2):
    total = None
    for _ in range(parts):
        piece = a.astype(BF16)
        a = a - piece.astype(F32)
        term = dot(piece, b)
        total = term if total is None else total + term
    return total


def split_right(a, b, parts=2):
    total = None
    for _ in range(parts):
        piece = b.astype(BF16)
        b = b - piece.astype(F32)
        term = dot(a, piece)
        total = term if total is None else total + term
    return total


def by_parity(odd, run, one, two):
    @pl.when(odd == 0)
    def _():
        run(one, two)

    @pl.when(odd == 1)
    def _():
        run(two, one)


def pack_rows_kernel(place, images_in, nodes_in, first_send, second_send, images, nodes, sems):
    copies = [pltpu.make_async_copy(nodes_in, nodes, sems.at[4])]
    for i in range(2):
        for k in range(2):
            part = (i, pl.ds(4 * k, 4))
            copies.append(
                pltpu.make_async_copy(images_in.at[part], images.at[part], sems.at[2 * i + k])
            )
    for copy in copies:
        copy.start()
    for copy in copies:
        copy.wait()

    def fill(last, first):
        for z in range(8):
            last[2 * z : 2 * z + 2, :] = images[0, z, 14:16, :]
            last[16 + z : 17 + z, :] = images[1, z, 15:16, :]
            first[2 * z : 2 * z + 2, :] = images[0, z, 0:2, :]
            first[16 + z : 17 + z, :] = images[1, z, 0:1, :]
        last[24:32, :] = jnp.zeros((8, 1024), F32)
        first[24:32, :] = jnp.zeros((8, 1024), F32)
        for c in range(3):
            first[24:25, 128 * c : 128 * c + 128] = nodes[c, 0, 0:1, :]

    by_parity(place[1] % 2, fill, first_send, second_send)


def pack_planes_kernel(place, images, nodes, first_rows, second_rows, first_send, second_send):
    def fill(forward, backward):
        for target, planes in ((forward, (6, 7, 7)), (backward, (0, 1, 0))):
            target[0:16, :] = images[0, planes[0]]
            target[16:32, :] = images[0, planes[1]]
            target[32:48, :] = images[1, planes[2]]
        forward[48:56, :] = jnp.zeros((8, 1024), F32)
        backward[48:56, :] = jnp.zeros((8, 1024), F32)

        def corners(high, low):
            for target, z in ((forward, 7), (backward, 0)):
                target[48:49, :] = low[16 + z : 17 + z, :]
                target[49:50, :] = high[16 + z : 17 + z, :]
            for c in range(3):
                for y in range(3):
                    i = c * 3 + y
                    source = nodes[c, 0, y : y + 1, :] if y < 2 else high[24:25, 128 * c : 128 * c + 128]
                    at = 128 * (i % 8)
                    backward[50 + i // 8 : 51 + i // 8, at : at + 128] = source

        by_parity(place[1] % 2, corners, first_rows, second_rows)

    by_parity(place[0] % 2, fill, first_send, second_send)


def shift_lanes(value, off):
    lane = lax.broadcasted_iota(jnp.int32, (1, 1024), 1)
    moved = pltpu.roll(value, (-off) % 1024, value.ndim - 1)
    inside = (lane + off >= 0) & (lane + off < 1024)
    return jnp.where(inside, moved, 0.0)


def inner_kernel(place, images, first_rows, second_rows, mid0, mid1, gx):
    mid0[:, 8:24, :] = images[0]
    mid1[1, :, 8:24, :] = images[1]

    def put_rows(high, low):
        for z in range(8):
            mid0[z, 6:8, :] = low[2 * z : 2 * z + 2, :]
            mid0[z, 24:26, :] = high[2 * z : 2 * z + 2, :]
            mid1[1, z, 7:8, :] = low[16 + z : 17 + z, :]
            mid1[1, z, 24:25, :] = high[16 + z : 17 + z, :]

    by_parity(place[1] % 2, put_rows, first_rows, second_rows)

    def along_x(z, carry):
        plane = mid1[1, z]
        mid1[0, z] = shift_lanes(plane, -1)
        mid1[2, z] = shift_lanes(plane, 1)
        t = images[0, z]
        near = shift_lanes(t, 1) - shift_lanes(t, -1)
        gx[z] = (shift_lanes(t, -2) - shift_lanes(t, 2) + 8.0 * near) * (1.0 / 12.0)
        return carry

    lax.fori_loop(0, 8, along_x, 0)


def inner_part(place, images, *rows):
    return pl.pallas_call(
        inner_kernel,
        out_shape=(
            jax.ShapeDtypeStruct((8, 32, 1024), F32),
            jax.ShapeDtypeStruct((3, 8, 32, 1024), F32),
            jax.ShapeDtypeStruct((8, 16, 1024), F32),
        ),
        in_specs=[SMEM] + [VMEM] * 3,
        out_specs=(VMEM,) * 3,
        compiler_params=pltpu.CompilerParams(vmem_limit_bytes=8 << 20),
        name="inner_part",
    )(place, images, *rows)


def local_kernel(
    place, mid0, mid1, gx, first_planes, second_planes, first_rows, second_rows, nodes,
    shifts_in, to_nodes_in, to_voxels_in, down_rows_in,
    mismatch, own, to_slab, to_plane,
    out0, out1, sh, un, acc, acc_rhs, near, shifts, to_nodes, to_voxels, down_rows, sems,
):
    pairs = (
        (shifts_in, shifts), (to_voxels_in, to_voxels), (to_nodes_in, to_nodes),
        (down_rows_in, down_rows),
    )
    copies = [pltpu.make_async_copy(a, b, sems.at[i]) for i, (a, b) in enumerate(pairs)]
    for copy in copies:
        copy.start()
    near[...] = jnp.zeros((24, 128), F32)
    for c in range(3):
        near[6 * c : 6 * c + 2, :] = nodes[c, 0]

    def put_planes(high, low):
        out0[0:2] = low[0:32, :].reshape(2, 16, 1024)
        out0[2:4] = high[0:32, :].reshape(2, 16, 1024)
        for k, source in ((0, low), (1, high)):
            out1[1, k, 8:24, :] = source[32:48, :]
            out1[1, k, 7:8, :] = source[48:49, :]
            out1[1, k, 24:25, :] = source[49:50, :]
        for c in range(3):
            for y in range(3):
                i = c * 3 + y
                at = 128 * (i % 8)
                r = 6 * c + 3 + y
                near[r : r + 1, :] = high[50 + i // 8 : 51 + i // 8, at : at + 128]

    def put_rows(high, low):
        for c in range(3):
            near[6 * c + 2 : 6 * c + 3, :] = high[24:25, 128 * c : 128 * c + 128]

    by_parity(place[0] % 2, put_planes, first_planes, second_planes)
    by_parity(place[1] % 2, put_rows, first_rows, second_rows)
    for k in range(2):
        plane = out1[1, k]
        out1[0, k] = shift_lanes(plane, -1)
        out1[2, k] = shift_lanes(plane, 1)
    copies[0].wait()
    copies[1].wait()
    for c in range(3):
        sh[2 * c : 2 * c + 2, :] = dot(shifts[c, 0].astype(F32).astype(BF16), to_voxels[128:256, :])
    un[...] = split_left(near[...], to_voxels[0:128, :], 3)
    wy = lax.broadcasted_iota(jnp.int32, (8, 128), 0).astype(F32) * 0.125

    def chunk(c, energy):
        at = pl.ds(pl.multiple_of(c * 128, 128), 128)
        for er in range(2):
            base = 8 + 8 * er

            def full(row):
                return jnp.broadcast_to(row, (8, 128))

            sz = full(sh[er : er + 1, at])
            sy = full(sh[2 + er : 3 + er, at])
            sx = full(sh[4 + er : 5 + er, at])
            x_low, x_up = sx < -0.5, sx > 0.5
            y_low, y_up = sy < -0.5, sy > 0.5
            z_low, z_up = sz < -0.5, sz > 0.5

            def in_plane(k):
                rows = []
                for dy in (-1, 0, 1):
                    ref, i = (mid1, k - 1) if 1 <= k <= 8 else (out1, k // 9)
                    a, b, d = (ref[n, i, base + dy : base + dy + 8, at] for n in range(3))
                    rows.append(jnp.where(x_low, a, jnp.where(x_up, d, b)))
                return jnp.where(y_low, rows[0], jnp.where(y_up, rows[2], rows[1]))

            corner = []
            for comp in range(3):
                for zn in range(2):
                    i = (comp * 2 + zn) * 3 + er
                    first, second = full(un[i : i + 1, at]), full(un[i + 1 : i + 2, at])
                    corner.append(first + wy * (second - first))
            sums = [None] * 18
            sums_rhs = [None] * 6
            planes = [in_plane(0), in_plane(1)]
            for z in range(8):
                planes.append(in_plane(z + 2))
                warped = jnp.where(z_low, planes[z], jnp.where(z_up, planes[z + 2], planes[z + 1]))

                def here(k):
                    if 2 <= k <= 9:
                        return mid0[k - 2, base : base + 8, at]
                    return out0[k if k < 2 else k - 8, base - 8 : base, at]

                rows = lambda dy: mid0[z, base + dy : base + dy + 8, at]
                g0 = (here(z) - here(z + 4) + 8.0 * (here(z + 3) - here(z + 1))) * (1.0 / 12.0)
                g1 = (rows(-2) - rows(2) + 8.0 * (rows(1) - rows(-1))) * (1.0 / 12.0)
                g2 = gx[z, base - 8 : base, at]
                g = (g0, g1, g2)
                w = z / 8.0
                total = None
                for comp in range(3):
                    moved = corner[2 * comp] + w * (corner[2 * comp + 1] - corner[2 * comp])
                    term = g[comp] * moved
                    total = term if total is None else total + term
                mis = here(z + 2) - warped - total
                mismatch[z, base - 8 : base, at] = mis

                def add(store, i, weight, value):
                    if weight:
                        term = value if weight == 1.0 else weight * value
                        store[i] = term if store[i] is None else store[i] + term

                for ab, (a, b) in enumerate(PAIRS):
                    prod = g[a] * g[b]
                    if a == b:
                        energy = energy + prod
                    for zt, weight in enumerate(((1 - w) * (1 - w), w * (1 - w), w * w)):
                        add(sums, zt * 6 + ab, weight, prod)
                for comp in range(3):
                    prod = g[comp] * mis
                    for zt, weight in enumerate((1 - w, w)):
                        add(sums_rhs, zt * 3 + comp, weight, prod)
            for i in range(18):
                r = (i * 2 + er) * 8
                acc[r : r + 8, at] = sums[i]
            for zt in range(2):
                for c in range(9):
                    r = ((zt * 9 + c) * 2 + er) * 8
                    if c < 3:
                        value = sums_rhs[zt * 3 + c]
                    else:
                        value = sums[zt * 6 + c - 3] + sums[zt * 6 + c + 3]
                    acc_rhs[r : r + 8, at] = value
        return energy

    energy = lax.fori_loop(0, NCHUNK, chunk, jnp.zeros((8, 128), F32))
    copies[2].wait()
    copies[3].wait()
    by_x = split_left(acc[...], to_nodes[:, 0:256])
    by_x_rhs = split_left(acc_rhs[...], to_nodes[:, 256:384])
    by_y = split_right(down_rows[0:192, :], by_x)
    by_y_rhs = split_right(down_rows[192:288, :], by_x_rhs)

    def edges(which, tx, first, count):
        r = 48 * which + first
        return by_y[r : r + count, 128 * tx : 128 * tx + 128]

    def whole(which, yl):
        r = 24 * which + 9 * yl
        return by_y_rhs[r + 3 : r + 9, :]

    def load(which, yl):
        r = 24 * which + 9 * yl
        return by_y_rhs[r : r + 3, :]

    own[0:6, :] = whole(0, 0)
    own[6:12, :] = whole(0, 1)
    own[12:48, :] = edges(0, 0, 12, 36)
    own[48:96, :] = edges(0, 1, 0, 48)
    own[96:99, :] = load(0, 0)
    own[99:102, :] = load(0, 1)
    own[108:112, :] = jnp.zeros((4, 128), F32)
    to_slab[0:6, :] = whole(1, 0)
    to_slab[6:12, :] = whole(1, 1)
    to_slab[12:24, :] = edges(1, 0, 12, 12)
    to_slab[24:48, :] = edges(1, 1, 0, 24)
    to_slab[48:51, :] = load(1, 0)
    to_slab[51:54, :] = load(1, 1)
    to_slab[54:56, :] = jnp.zeros((2, 128), F32)
    to_plane[0:6, :] = whole(2, 0)
    to_plane[6:12, :] = edges(2, 0, 24, 6)
    to_plane[12:18, :] = edges(2, 1, 0, 6)
    to_plane[18:24, :] = edges(2, 1, 24, 6)
    to_plane[24:30, :] = whole(3, 0)
    to_plane[30:36, :] = edges(3, 1, 0, 6)
    to_plane[36:39, :] = load(2, 0)
    to_plane[39:42, :] = load(3, 0)
    to_plane[42:48, :] = jnp.zeros((6, 128), F32)
    for yl in range(2):
        for comp in range(3):
            r = U_ROW + yl * 3 + comp
            own[r : r + 1, :] = nodes[comp, 0, yl : yl + 1, :]
    own[ENERGY_ROW : ENERGY_ROW + 1, :] = jnp.sum(energy, axis=0, keepdims=True)


VMEM = pl.BlockSpec(memory_space=pltpu.VMEM)
SMEM = pl.BlockSpec(memory_space=pltpu.SMEM)
HBM = pl.BlockSpec(memory_space=pltpu.HBM)


def in_hbm(array):
    return pltpu.with_memory_space_constraint(array, pltpu.HBM)


def pack_rows(place, images, nodes):
    message = jax.ShapeDtypeStruct((32, 1024), F32)
    return pl.pallas_call(
        pack_rows_kernel,
        out_shape=(
            message,
            message,
            jax.ShapeDtypeStruct(images.shape, F32),
            jax.ShapeDtypeStruct(nodes.shape, F32),
        ),
        in_specs=[SMEM, HBM, HBM],
        out_specs=(VMEM,) * 4,
        scratch_shapes=[pltpu.SemaphoreType.DMA((5,))],
        compiler_params=pltpu.CompilerParams(vmem_limit_bytes=4 << 20),
        name="pack_rows",
    )(place, in_hbm(images), in_hbm(nodes))


def pack_planes(place, *arrays):
    message = jax.ShapeDtypeStruct((56, 1024), F32)
    return pl.pallas_call(
        pack_planes_kernel,
        out_shape=(message, message),
        in_specs=[SMEM] + [VMEM] * len(arrays),
        out_specs=(VMEM, VMEM),
        compiler_params=pltpu.CompilerParams(vmem_limit_bytes=4 << 20),
        name="pack_planes",
    )(place, *arrays)


def local_part(place, *arrays):
    message = lambda rows: jax.ShapeDtypeStruct((rows, 128), F32)
    constants = build_constants()
    return pl.pallas_call(
        local_kernel,
        out_shape=(
            jax.ShapeDtypeStruct((8, 16, 1024), F32), message(ROWS), message(56), message(48)
        ),
        in_specs=[SMEM] + [VMEM] * 8 + [HBM] * 4,
        out_specs=(VMEM,) * 4,
        scratch_shapes=[
            pltpu.VMEM((4, 16, 1024), F32),
            pltpu.VMEM((3, 2, 32, 1024), F32),
            pltpu.VMEM((8, 1024), F32),
            pltpu.VMEM((24, 1024), F32),
            pltpu.VMEM((288, 1024), F32),
            pltpu.VMEM((288, 1024), F32),
            pltpu.VMEM((24, 128), F32),
            pltpu.VMEM((3, 1, 2, 128), jnp.int32),
            pltpu.VMEM((1024, 384), BF16),
            pltpu.VMEM((256, 1024), BF16),
            pltpu.VMEM((288, 288), BF16),
            pltpu.SemaphoreType.DMA((4,)),
        ],
        compiler_params=pltpu.CompilerParams(vmem_limit_bytes=12 << 20),
        name="local_part",
    )(place, *arrays[:-1], *(in_hbm(a) for a in (arrays[-1],) + constants))


def arrange(place, pieces, data):
    slab, plane = place[0], place[1]
    x_me, y_me = slab // 2, (slab % 2) * 2 + (plane // 2) % 2
    z_me, core = plane // 4, plane % 2

    def step(j, carry):
        bits = [(j >> i) & 1 for i in range(5)]
        for source, half, color, piece in pieces:
            k = core if source == 0 else 1 - core
            first, second = 3 - 2 * k, 1 + 2 * k
            start, count = COLORS[color]
            order = [(color + i) % 3 for i in range(3)]
            delta = [bits[0] * first, bits[1] * first, bits[2] * first]
            delta[order[0]] = delta[order[0]] ^ (bits[3] * second)
            delta[order[1]] = delta[order[1]] ^ (bits[4] * second)
            if half:
                delta[order[2]] = delta[order[2]] ^ second
            x, y, z = x_me ^ delta[0], y_me ^ delta[1], z_me ^ delta[2]
            device = (x * 2 + (y >> 1)) * 16 + z * 4 + (y & 1) * 2 + k
            for t in range(count // 8):
                r = (start + 8 * t) * STRIDE
                data[pl.ds(r + device, 8, stride=STRIDE), :] = piece[j, 8 * t : 8 * t + 8, :]
        return carry

    lax.fori_loop(0, 32, step, 0)


def early_kernel(*refs):
    place, pieces, data = refs[0], refs[1:7], refs[7]
    arrange(place, [(i // 3, 0, i % 3, pieces[i]) for i in range(6)], data)


def middle_kernel(*refs):
    place, pieces, data = refs[0], refs[2:5], refs[5]
    arrange(place, [(0, 1, i, pieces[i]) for i in range(3)], data)


def arranged(kernel, place, pieces, data=None):
    before = () if data is None else (data,)
    return pl.pallas_call(
        kernel,
        out_shape=jax.ShapeDtypeStruct((ROWS * STRIDE, 128), F32),
        in_specs=[SMEM] + [VMEM] * (len(before) + len(pieces)),
        out_specs=VMEM,
        input_output_aliases={} if data is None else {1: 0},
        compiler_params=pltpu.CompilerParams(vmem_limit_bytes=LIMIT_A),
    )(place, *before, *pieces)


def solve_kernel(*refs):
    place, nodes, _ = refs[:3]
    pieces = refs[3:6]
    out, data = refs[6:8]
    var, high, next_row, vec_x, vec_r, vec_p, vec_y = refs[8:]
    slab, plane = place[0], place[1]
    arrange(place, [(1, 1, i, pieces[i]) for i in range(3)], data)

    def field(r):
        return data[r * STRIDE : r * STRIDE + 128, :]

    total = jnp.sum(jnp.sum(field(ENERGY_ROW), axis=0, keepdims=True), axis=1, keepdims=True)
    penalty = reg_weight / (64.0 * 256.0 * 1024.0) * total

    def row_of(tx, tz, yk, ab):
        return ((tx * 2 + tz) * 4 + yk) * 6 + ab

    lane = lax.broadcasted_iota(jnp.int32, (128, 128), 1)
    row = lax.broadcasted_iota(jnp.int32, (128, 128), 0)
    in_plane = row % 16
    first = (lane == 0).astype(F32) + (row < 16).astype(F32)
    first = (first, first)
    first = (first[0] + (in_plane == 0).astype(F32), first[1])
    for ab in (0, 3, 5):
        for yl in range(2):
            for tx, tz, yk, weight in (
                (0, 0, yl, first[yl]), (0, 0, 2 + yl, -1.0), (0, 1, yl, -1.0), (1, 0, yl, -1.0)
            ):
                r = row_of(tx, tz, yk, ab) * STRIDE
                data[r : r + 128, :] = data[r : r + 128, :] + weight * penalty

    def x_next(v):
        return jnp.where(lane < 127, pltpu.roll(v, 127, 1), 0.0)

    def x_prev(v):
        return jnp.where(lane > 0, pltpu.roll(v, 1, 1), 0.0)

    def p_next(v):
        return jnp.where(in_plane < 15, pltpu.roll(v, 127, 0), 0.0)

    def p_prev(v):
        return jnp.where(in_plane > 0, pltpu.roll(v, 1, 0), 0.0)

    zero = jnp.zeros((16, 128), F32)

    def z_next(v):
        return jnp.concatenate([v[16:], zero], axis=0)

    def z_prev(v):
        return jnp.concatenate([zero, v[:112]], axis=0)

    for comp in range(3):
        u = [field(U_ROW + yl * 3 + comp) for yl in range(2)]
        for yl in range(2):
            v = u[yl]
            beside = z_next(v) + z_prev(v) + x_next(v) + x_prev(v)
            beside = beside + (u[1] + p_prev(u[1]) if yl == 0 else u[0] + p_next(u[0]))
            rhs = field(RHS_ROW + yl * 3 + comp) - penalty * (6.0 * v - beside)
            i = comp * 2 + yl
            vec_r[i] = rhs
            vec_p[i] = rhs
            vec_x[i] = jnp.zeros((128, 128), F32)

    def norm():
        value = None
        for i in range(6):
            term = vec_r[i] * vec_r[i]
            value = term if value is None else value + term
        return jnp.sum(jnp.sum(value, axis=0, keepdims=True), axis=1, keepdims=True)

    var[:, 128:144, :] = jnp.zeros((18, 16, 128), F32)
    lane8 = lax.broadcasted_iota(jnp.int32, (8, 128), 1)
    Y_CORNERS = ((0,), (1,), (0, 1), (1, 2))

    def multiply(i, carry):
        here = pl.ds(pl.multiple_of(i * 8, 8), 8)
        above = pl.ds(pl.multiple_of(i * 8 + 16, 8), 8)
        held = (i % 2) * 18
        values = {}
        for z in range(2):
            for b in range(3):
                for y in range(3):
                    for x in range(2):
                        k = (b * 3 + y) * 2 + x
                        values[z, y, x, b] = var[k, above if z else here, :]
        sums = {}

        def add(corner, a, value, sign=1):
            z, y, x = corner
            key = (z, y, x, a)
            if key not in sums:
                sums[key] = high[held + 3 * (y * 2 + x) + a] if z == 0 else None
            old = sums[key]
            if old is None:
                sums[key] = value if sign > 0 else -value
            else:
                sums[key] = old + value if sign > 0 else old - value

        def product(tx, tz, yk, v):
            m = []
            for ab in range(6):
                start = row_of(tx, tz, yk, ab) * STRIDE
                m.append(data[pl.ds(pl.multiple_of(start + i * 8, 8), 8), :])
            return [m[AB[a][0]] * v[0] + m[AB[a][1]] * v[1] + m[AB[a][2]] * v[2] for a in range(3)]

        for tz in range(2):
            for tx in range(2):
                for yk in range(4):
                    ys = Y_CORNERS[yk]
                    if tz == 0 and tx == 0 and yk < 2:
                        v = [values[0, ys[0], 0, b] for b in range(3)]
                        for a, q in enumerate(product(tx, tz, yk, v)):
                            add((0, ys[0], 0), a, q)
                        continue
                    ends = []
                    for oz in range(1 + tz):
                        for oy in range(len(ys)):
                            for ox in range(1 + tx):
                                one = (oz, ys[oy], ox)
                                two = (tz - oz, ys[len(ys) - 1 - oy], tx - ox)
                                if (two, one) not in ends:
                                    ends.append((one, two))
                    for one, two in ends:
                        v = [values[two + (b,)] - values[one + (b,)] for b in range(3)]
                        for a, q in enumerate(product(tx, tz, yk, v)):
                            add(one, a, q)
                            add(two, a, q, -1)
        for a in range(3):
            for y in range(3):
                part = sums[0, y, 0, a] + jnp.where(
                    lane8 > 0, pltpu.roll(sums[0, y, 1, a], 1, 1), 0.0
                )
                if y < 2:
                    vec_y[a * 2 + y, here, :] = part
                else:
                    next_row[a, here, :] = part
                for x in range(2):
                    high[held + 3 * (y * 2 + x) + a] = sums[1, y, x, a]
        return carry

    def apply():
        for comp in range(3):
            own = [vec_p[comp * 2 + yl] for yl in range(2)]
            for y_kind, v in enumerate((own[0], own[1], p_next(own[0]))):
                i = (comp * 3 + y_kind) * 2
                var[i, 0:128, :] = v
                var[i + 1, 0:128, :] = x_next(v)
        high[...] = jnp.zeros((36, 8, 128), F32)
        lax.fori_loop(0, 16, multiply, 0)
        energy = None
        for comp in range(3):
            vec_y[comp * 2] = vec_y[comp * 2] + p_prev(next_row[comp])
            for yl in range(2):
                term = vec_y[comp * 2 + yl] * vec_p[comp * 2 + yl]
                energy = term if energy is None else energy + term
        curvature = jnp.sum(jnp.sum(energy, axis=0, keepdims=True), axis=1, keepdims=True)
        return curvature

    def sweep(step, norm_now):
        size = norm_now / apply()
        for i in range(6):
            vec_x[i] = vec_x[i] + size * vec_p[i]
            vec_r[i] = vec_r[i] - size * vec_y[i]
        norm_next = norm()
        ratio = norm_next / norm_now
        for i in range(6):
            vec_p[i] = vec_r[i] + ratio * vec_p[i]
        return norm_next

    norm_last = lax.fori_loop(0, ITERS - 1, sweep, norm())
    size = norm_last / apply()
    mine = slab * 16 + plane
    for comp in range(3):
        for yl in range(2):
            out[comp, 0, yl : yl + 1, :] = (
                nodes[comp, 0, yl : yl + 1, :]
                + vec_x[comp * 2 + yl, pl.ds(mine, 1), :]
                + size * vec_p[comp * 2 + yl, pl.ds(mine, 1), :]
            )


def solve_part(place, nodes, data, pieces):
    return pl.pallas_call(
        solve_kernel,
        out_shape=(
            jax.ShapeDtypeStruct((3, 1, 2, 128), F32),
            jax.ShapeDtypeStruct((ROWS * STRIDE, 128), F32),
        ),
        in_specs=[SMEM] + [VMEM] * 5,
        out_specs=(VMEM, VMEM),
        input_output_aliases={2: 1},
        scratch_shapes=[
            pltpu.VMEM((18, 144, 128), F32),
            pltpu.VMEM((36, 8, 128), F32),
            pltpu.VMEM((3, 128, 128), F32),
        ]
        + [pltpu.VMEM((6, 128, 128), F32)] * 4,
        compiler_params=pltpu.CompilerParams(vmem_limit_bytes=LIMIT_B),
        name="solve_part",
    )(place, nodes, data, *pieces)[0]


def coordinates(device):
    slab, plane = divmod(device, 16)
    x, y_hi = divmod(slab, 2)
    z, rest = divmod(plane, 4)
    y_lo, core = divmod(rest, 2)
    return [x, y_hi * 2 + y_lo, z, core]


def device_of(x, y, z, core):
    return (x * 2 + y // 2) * 16 + z * 4 + (y % 2) * 2 + core


def exchange(value, axis, second):
    pairs = []
    for device in range(128):
        at = coordinates(device)
        if axis == 3:
            at[3] = 1 - at[3]
        else:
            at[axis] ^= 3 if (at[3] == 1) == second else 1
        pairs.append((device, device_of(*at)))
    return lax.ppermute(value, AXES, pairs)


def shifted(value, slab_step, plane_step):
    pairs = []
    for slab in range(8 - slab_step):
        for plane in range(16 - plane_step):
            pairs.append((slab * 16 + plane, (slab + slab_step) * 16 + plane + plane_step))
    return lax.ppermute(value, AXES, pairs)


def swap(value, axis, second):
    count = lax.axis_size(axis)
    pairs = []
    for i in range(count):
        j = i + (1 if (i % 2 == 1) == second else -1)
        if 0 <= j < count:
            pairs.append((i, j))
    return lax.ppermute(value, axis, pairs)


def program(images, shifts, nodes):
    place = jnp.stack([lax.axis_index("slab"), lax.axis_index("plane")]).astype(jnp.int32)
    first, second, images, nodes = pack_rows(place, images, nodes)
    rows = swap(first, "plane", False), swap(second, "plane", True)
    first, second = pack_planes(place, images, nodes, *rows)
    planes = swap(first, "slab", False), swap(second, "slab", True)
    inner = inner_part(place, images, *rows)
    mismatch, own, to_slab, to_plane = local_part(place, *inner, *planes, *rows, nodes, shifts)

    def spaced(value, layout):
        rows = []
        for start, count, gap in layout:
            rows += [value[start : start + count], jnp.zeros((gap, 128), F32)]
        return jnp.concatenate(rows, 0)

    got = shifted(to_plane, 0, 1)
    to_slab = to_slab + spaced(got, ((24, 6, 18), (30, 6, 18), (39, 3, 5)))
    own = own + spaced(got, ((0, 6, 18), (6, 6, 18), (12, 6, 18), (18, 6, 18), (36, 3, 13)))
    got = shifted(to_slab, 1, 0)
    payload = own + spaced(got, ((0, 24, 24), (24, 24, 24), (48, 6, 10)))
    blocks = payload[None]
    for axis in range(3):
        blocks = jnp.concatenate([blocks, exchange(blocks, axis, False)], 0)
    parts = [blocks[:, start : start + count] for start, count in COLORS]
    for turn in range(2):
        parts = [
            jnp.concatenate([part, exchange(part, (color + turn) % 3, True)], 0)
            for color, part in enumerate(parts)
        ]
    last = []
    for color, part in enumerate(parts):
        last.append(exchange(part, (color + 2) % 3, True))
    other = []
    for part in parts:
        other.append(exchange(part, 3, False))
    data = arranged(early_kernel, place, parts + other)
    data = arranged(middle_kernel, place, last, data)
    other = []
    for part in last:
        other.append(exchange(part, 3, False))
    result = solve_part(place, nodes, data, other)
    return result, mismatch


def solution(mesh):
    in_specs = (
        P(None, "slab", "plane", None),
        P(None, "slab", "plane", None),
        P(None, "slab", "plane", None),
    )
    out_specs = (P(None, "slab", "plane", None), P("slab", "plane", None))
    return jax.shard_map(program, mesh=mesh, in_specs=in_specs, out_specs=out_specs, check_vma=False)
```

profile of v0, /device:TPU:1, one launch (start us, length us, event | category | flops | bytes accessed | tf_op | source)
XLA Modules:
  0.0 123.7 jit_solution(15196174699067285371)
XLA Ops:
  0.6 0.1 pad_add_fusion.place.refs_0_
  0.7 1.9 %pack_rows.1 = (f32[32,1024]{1,0:T(8,128)S(1)}, f32[32,1024]{1,0:T(8,128)S(1)}, f32[2,8,16,1024]{3,2,1,0:T(8,128)S(1)}, f32[3,1,2,128]{3,2,1,0:T(2,128)S(1)}) custom-call(s32[2]{0:T(128)S(1)} %pad_add_fusion.place.refs_0_, f32[2,8,16,1024]{3,2,1,0:T(8,128)} %images_in.1, f32[3,1,2,128]{3,2,1,0:T(2,128)} %nodes_in.1), custom_call_target="tpu_custom_call" | custom-call | tf_op jit(solution)/shard_map/pack_rows/pallas_call | solution.py:408
  2.6 1.5 %collective-permute-start = (f32[32,1024]{1,0:T(8,128)S(1)}, f32[32,1024]{1,0:T(8,128)S(1)}, u32[]{:S(2)}, u32[]{:S(2)}) collective-permute-start(f32[32,1024]{1,0:T(8,128)S(1)} %get-tuple-element.18), channel_id=1, source_target_pairs={{0,1},{1,0},{2,3},{3,2},{4,5},{5,4},{6,7},{7,6},{8,9},{9,8},{10,11... | collective-permute-start | bytes 393224 | tf_op jit(solution)/shard_map/ppermute | solution.py:755
  4.0 3.2 %collective-permute-start.1 = (f32[32,1024]{1,0:T(8,128)S(1)}, f32[32,1024]{1,0:T(8,128)S(1)}, u32[]{:S(2)}, u32[]{:S(2)}) collective-permute-start(f32[32,1024]{1,0:T(8,128)S(1)} %get-tuple-element.19), channel_id=1, source_target_pairs={{1,2},{2,1},{3,4},{4,3},{5,6},{6,5},{7,8},{8,7},{9,10},{10,9},{11,... | collective-permute-start | bytes 393224 | tf_op jit(solution)/shard_map/ppermute | solution.py:755
  7.3 0.0 collective-permute-done.first_rows
  7.3 3.9 %collective-permute-done.1.second_rows = f32[32,1024]{1,0:T(8,128)S(1)} collective-permute-done((f32[32,1024]{1,0:T(8,128)S(1)}, f32[32,1024]{1,0:T(8,128)S(1)}, u32[]{:S(2)}, u32[]{:S(2)}) %collective-permute-start.1) | collective-permute-done | bytes 131104 | tf_op jit(solution)/shard_map/ppermute | solution.py:755
  11.2 0.6 pack_planes.1
  11.8 3.2 %collective-permute-start.2 = (f32[56,1024]{1,0:T(8,128)S(1)}, f32[56,1024]{1,0:T(8,128)S(1)}, u32[]{:S(2)}, u32[]{:S(2)}) collective-permute-start(f32[56,1024]{1,0:T(8,128)S(1)} %get-tuple-element.23), channel_id=1, source_target_pairs={{0,16},{16,0},{32,48},{48,32},{64,80},{80,64},{96,112},{112,96},{1... | collective-permute-start | bytes 688136 | tf_op jit(solution)/shard_map/ppermute | solution.py:755
  15.0 0.7 collective-permute-start.3
  15.7 2.3 %inner_part.1 = (f32[8,32,1024]{2,1,0:T(8,128)S(1)}, f32[3,8,32,1024]{3,2,1,0:T(8,128)S(1)}, f32[8,16,1024]{2,1,0:T(8,128)S(1)}) custom-call(s32[2]{0:T(128)S(1)} %pad_add_fusion.place.refs_0_, f32[2,8,16,1024]{3,2,1,0:T(8,128)S(1)} %get-tuple-element.17.images, f32[32,1024]{1,0:T(8,128)S(1)} %collective-permute-done.first_rows, ...), custom_call_target="tpu_custom_call" | custom-call | tf_op jit(solution)/shard_map/inner_part/pallas_call | solution.py:202
  18.0 0.4 collective-permute-done.2.first_planes
  18.4 6.2 %local_part.1 = (f32[8,16,1024]{2,1,0:T(8,128)}, f32[112,128]{1,0:T(8,128)S(1)}, f32[56,128]{1,0:T(8,128)S(1)}, f32[48,128]{1,0:T(8,128)S(1)}) custom-call(s32[2]{0:T(128)S(1)} %pad_add_fusion.place.refs_0_, f32[8,32,1024]{2,1,0:T(8,128)S(1)} %get-tuple-element.20.mid0, f32[3,8,32,1024]{3,2,1,0:T(8,128)S(1)} %get-tuple-element.21.mid1, ...), custom_call_target="tpu_custom_call" | custom-call | tf_op jit(solution)/shard_map/local_part/pallas_call | solution.py:439
  24.6 10.2 %collective-permute-start.4 = (f32[48,128]{1,0:T(8,128)S(1)}, f32[48,128]{1,0:T(8,128)S(1)}, u32[]{:S(2)}, u32[]{:S(2)}) collective-permute-start(f32[48,128]{1,0:T(8,128)S(1)} %get-tuple-element.26), channel_id=1, source_target_pairs={{0,1},{1,2},{2,3},{3,4},{4,5},{5,6},{6,7},{7,8},{8,9},{9,10},{10,1... | collective-permute-start | bytes 73736 | tf_op jit(solution)/shard_map/ppermute | solution.py:745
  34.8 0.9 collective-permute-done.4
  35.8 0.3 concatenate.42
  36.1 6.2 %collective-permute-start.5 = (f32[56,128]{1,0:T(8,128)S(1)}, f32[56,128]{1,0:T(8,128)S(1)}, u32[]{:S(2)}, u32[]{:S(2)}) collective-permute-start(f32[56,128]{1,0:T(8,128)S(1)} %add.10), channel_id=1, source_target_pairs={{0,16},{1,17},{2,18},{3,19},{4,20},{5,21},{6,22},{7,23},{8,24},{9,... | collective-permute-start | bytes 86024 | tf_op jit(solution)/shard_map/ppermute | solution.py:745
  42.3 0.7 concatenate.41
  43.0 0.3 collective-permute-done.5
  43.3 0.1 concatenate.43
  43.4 3.1 %collective-permute-start.6 = (f32[1,112,128]{2,1,0:T(8,128)S(1)}, f32[1,112,128]{2,1,0:T(8,128)S(1)}, u32[]{:S(2)}, u32[]{:S(2)}) collective-permute-start(f32[1,112,128]{2,1,0:T(8,128)S(1)} %add_bitcast_fusion), channel_id=1, source_target_pairs={{0,96},{1,33},{2,98},{3,35},{4,100},{5,37},{6,102},{7,39},{8,104},... | collective-permute-start | bytes 172040 | tf_op jit(solution)/shard_map/ppermute | solution.py:737
  46.5 1.6 %collective-permute-done.6 = f32[1,112,128]{2,1,0:T(8,128)S(1)} collective-permute-done((f32[1,112,128]{2,1,0:T(8,128)S(1)}, f32[1,112,128]{2,1,0:T(8,128)S(1)}, u32[]{:S(2)}, u32[]{:S(2)}) %collective-permute-start.6) | collective-permute-done | bytes 57376 | tf_op jit(solution)/shard_map/ppermute | solution.py:737
  48.1 1.4 %collective-permute-start.7 = (f32[2,112,128]{2,1,0:T(8,128)S(1)}, f32[2,112,128]{2,1,0:T(8,128)S(1)}, u32[]{:S(2)}, u32[]{:S(2)}) collective-permute-start(f32[2,112,128]{2,1,0:T(8,128)S(1)} %pad_maximum_fusion.9), channel_id=1, source_target_pairs={{0,18},{1,3},{2,16},{3,1},{4,22},{5,7},{6,20},{7,5},{8,26},{9,11},... | collective-permute-start | bytes 344072 | tf_op jit(solution)/shard_map/ppermute | solution.py:737
  49.5 2.3 %collective-permute-done.7 = f32[2,112,128]{2,1,0:T(8,128)S(1)} collective-permute-done((f32[2,112,128]{2,1,0:T(8,128)S(1)}, f32[2,112,128]{2,1,0:T(8,128)S(1)}, u32[]{:S(2)}, u32[]{:S(2)}) %collective-permute-start.7) | collective-permute-done | bytes 114720 | tf_op jit(solution)/shard_map/ppermute | solution.py:737
  51.9 2.1 %collective-permute-start.8 = (f32[4,112,128]{2,1,0:T(8,128)S(1)}, f32[4,112,128]{2,1,0:T(8,128)S(1)}, u32[]{:S(2)}, u32[]{:S(2)}) collective-permute-start(f32[4,112,128]{2,1,0:T(8,128)S(1)} %pad_maximum_fusion.7), channel_id=1, source_target_pairs={{0,12},{1,5},{2,14},{3,7},{4,8},{5,1},{6,10},{7,3},{8,4},{9,13},{1... | collective-permute-start | bytes 688136 | tf_op jit(solution)/shard_map/ppermute | solution.py:737
  54.0 3.4 %collective-permute-done.8 = f32[4,112,128]{2,1,0:T(8,128)S(1)} collective-permute-done((f32[4,112,128]{2,1,0:T(8,128)S(1)}, f32[4,112,128]{2,1,0:T(8,128)S(1)}, u32[]{:S(2)}, u32[]{:S(2)}) %collective-permute-start.8) | collective-permute-done | bytes 229408 | tf_op jit(solution)/shard_map/ppermute | solution.py:737
  57.5 1.9 %collective-permute-start.11 = (f32[8,40,128]{2,1,0:T(8,128)S(1)}, f32[8,40,128]{2,1,0:T(8,128)S(1)}, u32[]{:S(2)}, u32[]{:S(2)}) collective-permute-start(f32[8,40,128]{2,1,0:T(8,128)S(1)} %get-tuple-element.30), channel_id=1, source_target_pairs={{0,2},{1,19},{2,0},{3,17},{4,6},{5,23},{6,4},{7,21},{8,10},{9,27},... | collective-permute-start | bytes 491528 | tf_op jit(solution)/shard_map/ppermute | solution.py:737
  59.3 1.6 %collective-permute-start.9 = (f32[8,40,128]{2,1,0:T(8,128)S(1)}, f32[8,40,128]{2,1,0:T(8,128)S(1)}, u32[]{:S(2)}, u32[]{:S(2)}) collective-permute-start(f32[8,40,128]{2,1,0:T(8,128)S(1)} %get-tuple-element.31), channel_id=1, source_target_pairs={{0,32},{1,97},{2,34},{3,99},{4,36},{5,101},{6,38},{7,103},{8,40},{... | collective-permute-start | bytes 491528 | tf_op jit(solution)/shard_map/ppermute | solution.py:737
  60.9 2.0 %collective-permute-done.11 = f32[8,40,128]{2,1,0:T(8,128)S(1)} collective-permute-done((f32[8,40,128]{2,1,0:T(8,128)S(1)}, f32[8,40,128]{2,1,0:T(8,128)S(1)}, u32[]{:S(2)}, u32[]{:S(2)}) %collective-permute-start.11) | collective-permute-done | bytes 163872 | tf_op jit(solution)/shard_map/ppermute | solution.py:737
  62.9 2.2 %collective-permute-start.12 = (f32[16,40,128]{2,1,0:T(8,128)S(1)}, f32[16,40,128]{2,1,0:T(8,128)S(1)}, u32[]{:S(2)}, u32[]{:S(2)}) collective-permute-start(f32[16,40,128]{2,1,0:T(8,128)S(1)} %pad_maximum_fusion.5), channel_id=1, source_target_pairs={{0,4},{1,13},{2,6},{3,15},{4,0},{5,9},{6,2},{7,11},{8,12},{9,5},{1... | collective-permute-start | bytes 983048 | tf_op jit(solution)/shard_map/ppermute | solution.py:737
  65.1 0.7 collective-permute-start.13
  65.8 0.0 collective-permute-done.9
  65.8 1.9 %collective-permute-start.10 = (f32[16,40,128]{2,1,0:T(8,128)S(1)}, f32[16,40,128]{2,1,0:T(8,128)S(1)}, u32[]{:S(2)}, u32[]{:S(2)}) collective-permute-start(f32[16,40,128]{2,1,0:T(8,128)S(1)} %pad_maximum_fusion.4), channel_id=1, source_target_pairs={{0,2},{1,19},{2,0},{3,17},{4,6},{5,23},{6,4},{7,21},{8,10},{9,27},... | collective-permute-start | bytes 983048 | tf_op jit(solution)/shard_map/ppermute | solution.py:737
  67.7 4.5 %collective-permute-done.13 = f32[8,32,128]{2,1,0:T(8,128)S(1)} collective-permute-done((f32[8,32,128]{2,1,0:T(8,128)S(1)}, f32[8,32,128]{2,1,0:T(8,128)S(1)}, u32[]{:S(2)}, u32[]{:S(2)}) %collective-permute-start.13) | collective-permute-done | bytes 131104 | tf_op jit(solution)/shard_map/ppermute | solution.py:737
  72.2 3.0 %collective-permute-start.14 = (f32[16,32,128]{2,1,0:T(8,128)S(1)}, f32[16,32,128]{2,1,0:T(8,128)S(1)}, u32[]{:S(2)}, u32[]{:S(2)}) collective-permute-start(f32[16,32,128]{2,1,0:T(8,128)S(1)} %pad_maximum_fusion.6), channel_id=1, source_target_pairs={{0,32},{1,97},{2,34},{3,99},{4,36},{5,101},{6,38},{7,103},{8,40},{... | collective-permute-start | bytes 786440 | tf_op jit(solution)/shard_map/ppermute | solution.py:737
  75.3 0.1 collective-permute-start.19
  75.5 3.0 %collective-permute-start.18 = (f32[32,40,128]{2,1,0:T(8,128)S(1)}, f32[32,40,128]{2,1,0:T(8,128)S(1)}, u32[]{:S(2)}, u32[]{:S(2)}) collective-permute-start(f32[32,40,128]{2,1,0:T(8,128)S(1)} %pad_maximum_fusion.refs_1_), channel_id=1, source_target_pairs={{0,4},{1,13},{2,6},{3,15},{4,0},{5,9},{6,2},{7,11},{8,12},{9,5},{1... | collective-permute-start | bytes 1966088 | tf_op jit(solution)/shard_map/ppermute | solution.py:737
  78.5 0.5 collective-permute-done.14
  79.1 10.6 %collective-permute-start.17 = (f32[32,32,128]{2,1,0:T(8,128)S(1)}, f32[32,32,128]{2,1,0:T(8,128)S(1)}, u32[]{:S(2)}, u32[]{:S(2)}) collective-permute-start(f32[32,32,128]{2,1,0:T(8,128)S(1)} %pad_maximum_fusion.2.refs_3_), channel_id=1, source_target_pairs={{0,1},{1,0},{2,3},{3,2},{4,5},{5,4},{6,7},{7,6},{8,9},{9,8},{10,11... | collective-permute-start | bytes 1572872 | tf_op jit(solution)/shard_map/ppermute | solution.py:737
  89.7 0.2 collective-permute-start.16
  89.9 1.4 %collective-permute-done.17.refs_6_ = f32[32,32,128]{2,1,0:T(8,128)S(1)} collective-permute-done((f32[32,32,128]{2,1,0:T(8,128)S(1)}, f32[32,32,128]{2,1,0:T(8,128)S(1)}, u32[]{:S(2)}, u32[]{:S(2)}) %collective-permute-start.17) | collective-permute-done | bytes 524320 | tf_op jit(solution)/shard_map/ppermute | solution.py:737
  91.2 0.4 collective-permute-start.15
  91.6 5.0 %collective-permute-start.22 = (f32[32,40,128]{2,1,0:T(8,128)S(1)}, f32[32,40,128]{2,1,0:T(8,128)S(1)}, u32[]{:S(2)}, u32[]{:S(2)}) collective-permute-start(f32[32,40,128]{2,1,0:T(8,128)S(1)} %collective-permute-done.19.refs_3_), channel_id=1, source_target_pairs={{0,1},{1,0},{2,3},{3,2},{4,5},{5,4},{6,7},{7,6},{8,9},{9,8},{10,11... | collective-permute-start | bytes 1966088 | tf_op jit(solution)/shard_map/ppermute | solution.py:737
  96.6 0.0 collective-permute-start.21
  96.6 2.3 %collective-permute-done.20.refs_4_ = f32[32,32,128]{2,1,0:T(8,128)S(1)} collective-permute-done((f32[32,32,128]{2,1,0:T(8,128)S(1)}, f32[32,32,128]{2,1,0:T(8,128)S(1)}, u32[]{:S(2)}, u32[]{:S(2)}) %collective-permute-start.20) | collective-permute-done | bytes 524320 | tf_op jit(solution)/shard_map/ppermute | solution.py:737
  98.9 0.0 collective-permute-start.23
  99.0 2.6 %shard_map.77.refs_1_ = f32[15232,128]{1,0:T(8,128)S(1)} custom-call(s32[2]{0:T(128)S(1)} %pad_add_fusion.place.refs_0_, f32[32,40,128]{2,1,0:T(8,128)S(1)} %pad_maximum_fusion.refs_1_, f32[32,40,128]{2,1,0:T(8,128)S(1)} %pad_maximum_fusion.1.refs_2_, f32[32,32,128]{2,1,0:T(8,128)S(1)} %pad_maximum_fusion.2.refs_3_, ...), custom_call_target="tpu_custom_call" | custom-call | tf_op jit(solution)/shard_map/pallas_call | solution.py:504
  101.5 1.6 %shard_map.78.refs_2_ = f32[15232,128]{1,0:T(8,128)S(1)} custom-call(s32[2]{0:T(128)S(1)} %pad_add_fusion.place.refs_0_, f32[15232,128]{1,0:T(8,128)S(1)} %shard_map.77.refs_1_, f32[32,40,128]{2,1,0:T(8,128)S(1)} %collective-permute-done.18.refs_2_, f32[32,40,128]{2,1,0:T(8,128)S(1)} %collective-permute-done.19.refs_3_, ...), custom_call_target="tpu_custom_call", output_to_operand_aliasing={{}: (1, {})} | custom-call | tf_op jit(solution)/shard_map/pallas_call | solution.py:504
  103.2 20.6 %solve_part.1 = (f32[3,1,2,128]{3,2,1,0:T(2,128)}, f32[15232,128]{1,0:T(8,128)S(1)}) custom-call(s32[2]{0:T(128)S(1)} %pad_add_fusion.place.refs_0_, f32[3,1,2,128]{3,2,1,0:T(2,128)S(1)} %get-tuple-element.16.nodes.refs_1_, f32[15232,128]{1,0:T(8,128)S(1)} %shard_map.78.refs_2_, ...), custom_call_target="tpu_custom_call", output_to_operand_aliasing={{1}: (2, {})} | custom-call | tf_op jit(solution)/shard_map/solve_part/pallas_call | solution.py:696
  (33 shorter events, 0.4 us)
Async XLA Ops:
  2.6 4.7 %collective-permute-start = (f32[32,1024]{1,0:T(8,128)S(1)}, f32[32,1024]{1,0:T(8,128)S(1)}, u32[]{:S(2)}, u32[]{:S(2)}) collective-permute-start(f32[32,1024]{1,0:T(8,128)S(1)} %get-tuple-element.18), channel_id=1, source_target_pairs={{0,1},{1,0},{2,3},{3,2},{4,5},{5,4},{6,7},{7,6},{8,9},{9,8},{10,11... | collective-permute-start | bytes 393224 | tf_op jit(solution)/shard_map/ppermute | solution.py:755
  4.0 7.2 %collective-permute-start.1 = (f32[32,1024]{1,0:T(8,128)S(1)}, f32[32,1024]{1,0:T(8,128)S(1)}, u32[]{:S(2)}, u32[]{:S(2)}) collective-permute-start(f32[32,1024]{1,0:T(8,128)S(1)} %get-tuple-element.19), channel_id=1, source_target_pairs={{1,2},{2,1},{3,4},{4,3},{5,6},{6,5},{7,8},{8,7},{9,10},{10,9},{11,... | collective-permute-start | bytes 393224 | tf_op jit(solution)/shard_map/ppermute | solution.py:755
  11.8 6.6 %collective-permute-start.2 = (f32[56,1024]{1,0:T(8,128)S(1)}, f32[56,1024]{1,0:T(8,128)S(1)}, u32[]{:S(2)}, u32[]{:S(2)}) collective-permute-start(f32[56,1024]{1,0:T(8,128)S(1)} %get-tuple-element.23), channel_id=1, source_target_pairs={{0,16},{16,0},{32,48},{48,32},{64,80},{80,64},{96,112},{112,96},{1... | collective-permute-start | bytes 688136 | tf_op jit(solution)/shard_map/ppermute | solution.py:755
  15.0 3.4 %collective-permute-start.3 = (f32[56,1024]{1,0:T(8,128)S(1)}, f32[56,1024]{1,0:T(8,128)S(1)}, u32[]{:S(2)}, u32[]{:S(2)}) collective-permute-start(f32[56,1024]{1,0:T(8,128)S(1)} %get-tuple-element.24), channel_id=1, source_target_pairs={{16,32},{32,16},{48,64},{64,48},{80,96},{96,80},{17,33},{33,17},{4... | collective-permute-start | bytes 688136 | tf_op jit(solution)/shard_map/ppermute | solution.py:755
  24.6 11.1 %collective-permute-start.4 = (f32[48,128]{1,0:T(8,128)S(1)}, f32[48,128]{1,0:T(8,128)S(1)}, u32[]{:S(2)}, u32[]{:S(2)}) collective-permute-start(f32[48,128]{1,0:T(8,128)S(1)} %get-tuple-element.26), channel_id=1, source_target_pairs={{0,1},{1,2},{2,3},{3,4},{4,5},{5,6},{6,7},{7,8},{8,9},{9,10},{10,1... | collective-permute-start | bytes 73736 | tf_op jit(solution)/shard_map/ppermute | solution.py:745
  36.1 7.2 %collective-permute-start.5 = (f32[56,128]{1,0:T(8,128)S(1)}, f32[56,128]{1,0:T(8,128)S(1)}, u32[]{:S(2)}, u32[]{:S(2)}) collective-permute-start(f32[56,128]{1,0:T(8,128)S(1)} %add.10), channel_id=1, source_target_pairs={{0,16},{1,17},{2,18},{3,19},{4,20},{5,21},{6,22},{7,23},{8,24},{9,... | collective-permute-start | bytes 86024 | tf_op jit(solution)/shard_map/ppermute | solution.py:745
  43.4 4.7 %collective-permute-start.6 = (f32[1,112,128]{2,1,0:T(8,128)S(1)}, f32[1,112,128]{2,1,0:T(8,128)S(1)}, u32[]{:S(2)}, u32[]{:S(2)}) collective-permute-start(f32[1,112,128]{2,1,0:T(8,128)S(1)} %add_bitcast_fusion), channel_id=1, source_target_pairs={{0,96},{1,33},{2,98},{3,35},{4,100},{5,37},{6,102},{7,39},{8,104},... | collective-permute-start | bytes 172040 | tf_op jit(solution)/shard_map/ppermute | solution.py:737
  48.1 3.7 %collective-permute-start.7 = (f32[2,112,128]{2,1,0:T(8,128)S(1)}, f32[2,112,128]{2,1,0:T(8,128)S(1)}, u32[]{:S(2)}, u32[]{:S(2)}) collective-permute-start(f32[2,112,128]{2,1,0:T(8,128)S(1)} %pad_maximum_fusion.9), channel_id=1, source_target_pairs={{0,18},{1,3},{2,16},{3,1},{4,22},{5,7},{6,20},{7,5},{8,26},{9,11},... | collective-permute-start | bytes 344072 | tf_op jit(solution)/shard_map/ppermute | solution.py:737
  51.9 5.5 %collective-permute-start.8 = (f32[4,112,128]{2,1,0:T(8,128)S(1)}, f32[4,112,128]{2,1,0:T(8,128)S(1)}, u32[]{:S(2)}, u32[]{:S(2)}) collective-permute-start(f32[4,112,128]{2,1,0:T(8,128)S(1)} %pad_maximum_fusion.7), channel_id=1, source_target_pairs={{0,12},{1,5},{2,14},{3,7},{4,8},{5,1},{6,10},{7,3},{8,4},{9,13},{1... | collective-permute-start | bytes 688136 | tf_op jit(solution)/shard_map/ppermute | solution.py:737
  57.5 5.5 %collective-permute-start.11 = (f32[8,40,128]{2,1,0:T(8,128)S(1)}, f32[8,40,128]{2,1,0:T(8,128)S(1)}, u32[]{:S(2)}, u32[]{:S(2)}) collective-permute-start(f32[8,40,128]{2,1,0:T(8,128)S(1)} %get-tuple-element.30), channel_id=1, source_target_pairs={{0,2},{1,19},{2,0},{3,17},{4,6},{5,23},{6,4},{7,21},{8,10},{9,27},... | collective-permute-start | bytes 491528 | tf_op jit(solution)/shard_map/ppermute | solution.py:737
  59.3 6.5 %collective-permute-start.9 = (f32[8,40,128]{2,1,0:T(8,128)S(1)}, f32[8,40,128]{2,1,0:T(8,128)S(1)}, u32[]{:S(2)}, u32[]{:S(2)}) collective-permute-start(f32[8,40,128]{2,1,0:T(8,128)S(1)} %get-tuple-element.31), channel_id=1, source_target_pairs={{0,32},{1,97},{2,34},{3,99},{4,36},{5,101},{6,38},{7,103},{8,40},{... | collective-permute-start | bytes 491528 | tf_op jit(solution)/shard_map/ppermute | solution.py:737
  62.9 12.3 %collective-permute-start.12 = (f32[16,40,128]{2,1,0:T(8,128)S(1)}, f32[16,40,128]{2,1,0:T(8,128)S(1)}, u32[]{:S(2)}, u32[]{:S(2)}) collective-permute-start(f32[16,40,128]{2,1,0:T(8,128)S(1)} %pad_maximum_fusion.5), channel_id=1, source_target_pairs={{0,4},{1,13},{2,6},{3,15},{4,0},{5,9},{6,2},{7,11},{8,12},{9,5},{1... | collective-permute-start | bytes 983048 | tf_op jit(solution)/shard_map/ppermute | solution.py:737
  65.1 7.1 %collective-permute-start.13 = (f32[8,32,128]{2,1,0:T(8,128)S(1)}, f32[8,32,128]{2,1,0:T(8,128)S(1)}, u32[]{:S(2)}, u32[]{:S(2)}) collective-permute-start(f32[8,32,128]{2,1,0:T(8,128)S(1)} %pad_maximum_fusion.8), channel_id=1, source_target_pairs={{0,4},{1,13},{2,6},{3,15},{4,0},{5,9},{6,2},{7,11},{8,12},{9,5},{1... | collective-permute-start | bytes 393224 | tf_op jit(solution)/shard_map/ppermute | solution.py:737
  65.8 9.6 %collective-permute-start.10 = (f32[16,40,128]{2,1,0:T(8,128)S(1)}, f32[16,40,128]{2,1,0:T(8,128)S(1)}, u32[]{:S(2)}, u32[]{:S(2)}) collective-permute-start(f32[16,40,128]{2,1,0:T(8,128)S(1)} %pad_maximum_fusion.4), channel_id=1, source_target_pairs={{0,2},{1,19},{2,0},{3,17},{4,6},{5,23},{6,4},{7,21},{8,10},{9,27},... | collective-permute-start | bytes 983048 | tf_op jit(solution)/shard_map/ppermute | solution.py:737
  72.2 6.8 %collective-permute-start.14 = (f32[16,32,128]{2,1,0:T(8,128)S(1)}, f32[16,32,128]{2,1,0:T(8,128)S(1)}, u32[]{:S(2)}, u32[]{:S(2)}) collective-permute-start(f32[16,32,128]{2,1,0:T(8,128)S(1)} %pad_maximum_fusion.6), channel_id=1, source_target_pairs={{0,32},{1,97},{2,34},{3,99},{4,36},{5,101},{6,38},{7,103},{8,40},{... | collective-permute-start | bytes 786440 | tf_op jit(solution)/shard_map/ppermute | solution.py:737
  75.3 16.3 %collective-permute-start.19 = (f32[32,40,128]{2,1,0:T(8,128)S(1)}, f32[32,40,128]{2,1,0:T(8,128)S(1)}, u32[]{:S(2)}, u32[]{:S(2)}) collective-permute-start(f32[32,40,128]{2,1,0:T(8,128)S(1)} %pad_maximum_fusion.1.refs_2_), channel_id=1, source_target_pairs={{0,32},{1,97},{2,34},{3,99},{4,36},{5,101},{6,38},{7,103},{8,40},{... | collective-permute-start | bytes 1966088 | tf_op jit(solution)/shard_map/ppermute | solution.py:737
  75.5 21.1 %collective-permute-start.18 = (f32[32,40,128]{2,1,0:T(8,128)S(1)}, f32[32,40,128]{2,1,0:T(8,128)S(1)}, u32[]{:S(2)}, u32[]{:S(2)}) collective-permute-start(f32[32,40,128]{2,1,0:T(8,128)S(1)} %pad_maximum_fusion.refs_1_), channel_id=1, source_target_pairs={{0,4},{1,13},{2,6},{3,15},{4,0},{5,9},{6,2},{7,11},{8,12},{9,5},{1... | collective-permute-start | bytes 1966088 | tf_op jit(solution)/shard_map/ppermute | solution.py:737
  79.1 12.1 %collective-permute-start.17 = (f32[32,32,128]{2,1,0:T(8,128)S(1)}, f32[32,32,128]{2,1,0:T(8,128)S(1)}, u32[]{:S(2)}, u32[]{:S(2)}) collective-permute-start(f32[32,32,128]{2,1,0:T(8,128)S(1)} %pad_maximum_fusion.2.refs_3_), channel_id=1, source_target_pairs={{0,1},{1,0},{2,3},{3,2},{4,5},{5,4},{6,7},{7,6},{8,9},{9,8},{10,11... | collective-permute-start | bytes 1572872 | tf_op jit(solution)/shard_map/ppermute | solution.py:737
  89.7 9.2 %collective-permute-start.20 = (f32[32,32,128]{2,1,0:T(8,128)S(1)}, f32[32,32,128]{2,1,0:T(8,128)S(1)}, u32[]{:S(2)}, u32[]{:S(2)}) collective-permute-start(f32[32,32,128]{2,1,0:T(8,128)S(1)} %pad_maximum_fusion.2.refs_3_), channel_id=1, source_target_pairs={{0,2},{1,19},{2,0},{3,17},{4,6},{5,23},{6,4},{7,21},{8,10},{9,27},... | collective-permute-start | bytes 1572872 | tf_op jit(solution)/shard_map/ppermute | solution.py:737
  89.7 9.3 %collective-permute-start.16 = (f32[32,40,128]{2,1,0:T(8,128)S(1)}, f32[32,40,128]{2,1,0:T(8,128)S(1)}, u32[]{:S(2)}, u32[]{:S(2)}) collective-permute-start(f32[32,40,128]{2,1,0:T(8,128)S(1)} %pad_maximum_fusion.1.refs_2_), channel_id=1, source_target_pairs={{0,1},{1,0},{2,3},{3,2},{4,5},{5,4},{6,7},{7,6},{8,9},{9,8},{10,11... | collective-permute-start | bytes 1966088 | tf_op jit(solution)/shard_map/ppermute | solution.py:737
  91.2 7.7 %collective-permute-start.15 = (f32[32,40,128]{2,1,0:T(8,128)S(1)}, f32[32,40,128]{2,1,0:T(8,128)S(1)}, u32[]{:S(2)}, u32[]{:S(2)}) collective-permute-start(f32[32,40,128]{2,1,0:T(8,128)S(1)} %pad_maximum_fusion.refs_1_), channel_id=1, source_target_pairs={{0,1},{1,0},{2,3},{3,2},{4,5},{5,4},{6,7},{7,6},{8,9},{9,8},{10,11... | collective-permute-start | bytes 1966088 | tf_op jit(solution)/shard_map/ppermute | solution.py:737
  91.6 11.6 %collective-permute-start.22 = (f32[32,40,128]{2,1,0:T(8,128)S(1)}, f32[32,40,128]{2,1,0:T(8,128)S(1)}, u32[]{:S(2)}, u32[]{:S(2)}) collective-permute-start(f32[32,40,128]{2,1,0:T(8,128)S(1)} %collective-permute-done.19.refs_3_), channel_id=1, source_target_pairs={{0,1},{1,0},{2,3},{3,2},{4,5},{5,4},{6,7},{7,6},{8,9},{9,8},{10,11... | collective-permute-start | bytes 1966088 | tf_op jit(solution)/shard_map/ppermute | solution.py:737
  96.6 6.6 %collective-permute-start.21 = (f32[32,40,128]{2,1,0:T(8,128)S(1)}, f32[32,40,128]{2,1,0:T(8,128)S(1)}, u32[]{:S(2)}, u32[]{:S(2)}) collective-permute-start(f32[32,40,128]{2,1,0:T(8,128)S(1)} %collective-permute-done.18.refs_2_), channel_id=1, source_target_pairs={{0,1},{1,0},{2,3},{3,2},{4,5},{5,4},{6,7},{7,6},{8,9},{9,8},{10,11... | collective-permute-start | bytes 1966088 | tf_op jit(solution)/shard_map/ppermute | solution.py:737
  98.9 4.2 %collective-permute-start.23 = (f32[32,32,128]{2,1,0:T(8,128)S(1)}, f32[32,32,128]{2,1,0:T(8,128)S(1)}, u32[]{:S(2)}, u32[]{:S(2)}) collective-permute-start(f32[32,32,128]{2,1,0:T(8,128)S(1)} %collective-permute-done.20.refs_4_), channel_id=1, source_target_pairs={{0,1},{1,0},{2,3},{3,2},{4,5},{5,4},{6,7},{7,6},{8,9},{9,8},{10,11... | collective-permute-start | bytes 1572872 | tf_op jit(solution)/shard_map/ppermute | solution.py:737
where the time goes:
time: 124 us
  starting transfers between devices  62.1 us (50%)
  Pallas kernels  35.7 us (29%)
  waiting for transfers between devices  23.6 us (19%)
    ppermute x18, starting transfers between devices, exchange(): return lax.ppermute(value, AXES, pairs)  37.1 us
    pallas_call x1, Pallas kernels, solve_part(): pl.pallas_call(solve_kernel, out_shape=(jax.ShapeDtypeStruct((3, 1, 2, 12...  20.6 us
    ppermute x18, waiting for transfers between devices, exchange(): return lax.ppermute(value, AXES, pairs)  18.1 us
    ppermute x2, starting transfers between devices, shifted(): return lax.ppermute(value, AXES, pairs)  16.4 us
    ppermute x4, starting transfers between devices, swap(): return lax.ppermute(value, axis, pairs)  8.56 us
    pallas_call x1, Pallas kernels, local_part(): pl.pallas_call(local_kernel, out_shape=(jax.ShapeDtypeStruct((8, 16, 1024...  6.17 us
    ppermute x4, waiting for transfers between devices, swap(): return lax.ppermute(value, axis, pairs)  4.33 us
    pallas_call x2, Pallas kernels, arranged(): pl.pallas_call(kernel, out_shape=jax.ShapeDtypeStruct((ROWS * STRIDE, 128...  4.17 us
  transfers between devices with their start and end apart: 24, of which 12 were waited for; matrix products, arithmetic and copies ran while one was open for 1% of the time, Pallas kernels for 5%

commit v1 on v0

--- a/solution.py
+++ b/solution.py
@@ -651,7 +651,7 @@
                     high[held + 3 * (y * 2 + x) + a] = sums[1, y, x, a]
         return carry
 
-    def apply():
+    def sweep(step, norm_now):
         for comp in range(3):
             own = [vec_p[comp * 2 + yl] for yl in range(2)]
             for y_kind, v in enumerate((own[0], own[1], p_next(own[0]))):
@@ -659,7 +659,7 @@
                 var[i, 0:128, :] = v
                 var[i + 1, 0:128, :] = x_next(v)
         high[...] = jnp.zeros((36, 8, 128), F32)
-        lax.fori_loop(0, 16, multiply, 0)
+        lax.fori_loop(0, 16, multiply, 0, unroll=2)
         energy = None
         for comp in range(3):
             vec_y[comp * 2] = vec_y[comp * 2] + p_prev(next_row[comp])
@@ -667,10 +667,7 @@
                 term = vec_y[comp * 2 + yl] * vec_p[comp * 2 + yl]
                 energy = term if energy is None else energy + term
         curvature = jnp.sum(jnp.sum(energy, axis=0, keepdims=True), axis=1, keepdims=True)
-        return curvature
-
-    def sweep(step, norm_now):
-        size = norm_now / apply()
+        size = norm_now / curvature
         for i in range(6):
             vec_x[i] = vec_x[i] + size * vec_p[i]
             vec_r[i] = vec_r[i] - size * vec_y[i]
@@ -680,15 +677,12 @@
             vec_p[i] = vec_r[i] + ratio * vec_p[i]
         return norm_next
 
-    norm_last = lax.fori_loop(0, ITERS - 1, sweep, norm())
-    size = norm_last / apply()
+    lax.fori_loop(0, ITERS, sweep, norm())
     mine = slab * 16 + plane
     for comp in range(3):
         for yl in range(2):
             out[comp, 0, yl : yl + 1, :] = (
-                nodes[comp, 0, yl : yl + 1, :]
-                + vec_x[comp * 2 + yl, pl.ds(mine, 1), :]
-                + size * vec_p[comp * 2 + yl, pl.ds(mine, 1), :]
+                nodes[comp, 0, yl : yl + 1, :] + vec_x[comp * 2 + yl, pl.ds(mine, 1), :]
             )
 
 

time: 124 us -> 121 us (0.976)
  Pallas kernels: 35.7 us -> 32.7 us
    pallas_call x1, Pallas kernels: 20.6 us -> 17.5 us  [solve_part(): pl.pallas_call(solve_kernel, out_shape=(jax.ShapeDtypeStruct((3, 1, 2, 12...]
where the time goes in v1:
time: 121 us
  starting transfers between devices  62.1 us (51%)
  Pallas kernels  32.7 us (27%)
  waiting for transfers between devices  23.6 us (20%)
    ppermute x18, starting transfers between devices, exchange(): return lax.ppermute(value, AXES, pairs)  37.1 us
    ppermute x18, waiting for transfers between devices, exchange(): return lax.ppermute(value, AXES, pairs)  18.1 us
    pallas_call x1, Pallas kernels, solve_part(): pl.pallas_call(solve_kernel, out_shape=(jax.ShapeDtypeStruct((3, 1, 2, 12...  17.5 us
    ppermute x2, starting transfers between devices, shifted(): return lax.ppermute(value, AXES, pairs)  16.4 us
    ppermute x4, starting transfers between devices, swap(): return lax.ppermute(value, axis, pairs)  8.56 us
    pallas_call x1, Pallas kernels, local_part(): pl.pallas_call(local_kernel, out_shape=(jax.ShapeDtypeStruct((8, 16, 1024...  6.17 us
    ppermute x4, waiting for transfers between devices, swap(): return lax.ppermute(value, axis, pairs)  4.33 us
    pallas_call x2, Pallas kernels, arranged(): pl.pallas_call(kernel, out_shape=jax.ShapeDtypeStruct((ROWS * STRIDE, 128...  4.17 us
  transfers between devices with their start and end apart: 24, of which 12 were waited for; matrix products, arithmetic and copies ran while one was open for 1% of the time, Pallas kernels for 5%

profile of v1, /device:TPU:1, one launch (start us, length us, event | category | flops | bytes accessed | tf_op | source)
XLA Modules:
  0.0 120.7 jit_solution(13061611184243770098)
XLA Ops:
  0.6 0.1 pad_add_fusion.place.refs_0_
  0.7 1.9 %pack_rows.1 = (f32[32,1024]{1,0:T(8,128)S(1)}, f32[32,1024]{1,0:T(8,128)S(1)}, f32[2,8,16,1024]{3,2,1,0:T(8,128)S(1)}, f32[3,1,2,128]{3,2,1,0:T(2,128)S(1)}) custom-call(s32[2]{0:T(128)S(1)} %pad_add_fusion.place.refs_0_, f32[2,8,16,1024]{3,2,1,0:T(8,128)} %images_in.1, f32[3,1,2,128]{3,2,1,0:T(2,128)} %nodes_in.1), custom_call_target="tpu_custom_call" | custom-call | tf_op jit(solution)/shard_map/pack_rows/pallas_call | solution.py:408
  2.6 1.5 %collective-permute-start = (f32[32,1024]{1,0:T(8,128)S(1)}, f32[32,1024]{1,0:T(8,128)S(1)}, u32[]{:S(2)}, u32[]{:S(2)}) collective-permute-start(f32[32,1024]{1,0:T(8,128)S(1)} %get-tuple-element.18), channel_id=1, source_target_pairs={{0,1},{1,0},{2,3},{3,2},{4,5},{5,4},{6,7},{7,6},{8,9},{9,8},{10,11... | collective-permute-start | bytes 393224 | tf_op jit(solution)/shard_map/ppermute | solution.py:749
  4.0 3.2 %collective-permute-start.1 = (f32[32,1024]{1,0:T(8,128)S(1)}, f32[32,1024]{1,0:T(8,128)S(1)}, u32[]{:S(2)}, u32[]{:S(2)}) collective-permute-start(f32[32,1024]{1,0:T(8,128)S(1)} %get-tuple-element.19), channel_id=1, source_target_pairs={{1,2},{2,1},{3,4},{4,3},{5,6},{6,5},{7,8},{8,7},{9,10},{10,9},{11,... | collective-permute-start | bytes 393224 | tf_op jit(solution)/shard_map/ppermute | solution.py:749
  7.3 0.0 collective-permute-done.first_rows
  7.3 3.9 %collective-permute-done.1.second_rows = f32[32,1024]{1,0:T(8,128)S(1)} collective-permute-done((f32[32,1024]{1,0:T(8,128)S(1)}, f32[32,1024]{1,0:T(8,128)S(1)}, u32[]{:S(2)}, u32[]{:S(2)}) %collective-permute-start.1) | collective-permute-done | bytes 131104 | tf_op jit(solution)/shard_map/ppermute | solution.py:749
  11.2 0.6 pack_planes.1
  11.8 3.2 %collective-permute-start.2 = (f32[56,1024]{1,0:T(8,128)S(1)}, f32[56,1024]{1,0:T(8,128)S(1)}, u32[]{:S(2)}, u32[]{:S(2)}) collective-permute-start(f32[56,1024]{1,0:T(8,128)S(1)} %get-tuple-element.23), channel_id=1, source_target_pairs={{0,16},{16,0},{32,48},{48,32},{64,80},{80,64},{96,112},{112,96},{1... | collective-permute-start | bytes 688136 | tf_op jit(solution)/shard_map/ppermute | solution.py:749
  15.0 0.7 collective-permute-start.3
  15.7 2.3 %inner_part.1 = (f32[8,32,1024]{2,1,0:T(8,128)S(1)}, f32[3,8,32,1024]{3,2,1,0:T(8,128)S(1)}, f32[8,16,1024]{2,1,0:T(8,128)S(1)}) custom-call(s32[2]{0:T(128)S(1)} %pad_add_fusion.place.refs_0_, f32[2,8,16,1024]{3,2,1,0:T(8,128)S(1)} %get-tuple-element.17.images, f32[32,1024]{1,0:T(8,128)S(1)} %collective-permute-done.first_rows, ...), custom_call_target="tpu_custom_call" | custom-call | tf_op jit(solution)/shard_map/inner_part/pallas_call | solution.py:202
  18.0 0.4 collective-permute-done.2.first_planes
  18.4 6.2 %local_part.1 = (f32[8,16,1024]{2,1,0:T(8,128)}, f32[112,128]{1,0:T(8,128)S(1)}, f32[56,128]{1,0:T(8,128)S(1)}, f32[48,128]{1,0:T(8,128)S(1)}) custom-call(s32[2]{0:T(128)S(1)} %pad_add_fusion.place.refs_0_, f32[8,32,1024]{2,1,0:T(8,128)S(1)} %get-tuple-element.20.mid0, f32[3,8,32,1024]{3,2,1,0:T(8,128)S(1)} %get-tuple-element.21.mid1, ...), custom_call_target="tpu_custom_call" | custom-call | tf_op jit(solution)/shard_map/local_part/pallas_call | solution.py:439
  24.6 10.2 %collective-permute-start.4 = (f32[48,128]{1,0:T(8,128)S(1)}, f32[48,128]{1,0:T(8,128)S(1)}, u32[]{:S(2)}, u32[]{:S(2)}) collective-permute-start(f32[48,128]{1,0:T(8,128)S(1)} %get-tuple-element.26), channel_id=1, source_target_pairs={{0,1},{1,2},{2,3},{3,4},{4,5},{5,6},{6,7},{7,8},{8,9},{9,10},{10,1... | collective-permute-start | bytes 73736 | tf_op jit(solution)/shard_map/ppermute | solution.py:739
  34.8 0.9 collective-permute-done.4
  35.8 0.3 concatenate.42
  36.1 6.2 %collective-permute-start.5 = (f32[56,128]{1,0:T(8,128)S(1)}, f32[56,128]{1,0:T(8,128)S(1)}, u32[]{:S(2)}, u32[]{:S(2)}) collective-permute-start(f32[56,128]{1,0:T(8,128)S(1)} %add.10), channel_id=1, source_target_pairs={{0,16},{1,17},{2,18},{3,19},{4,20},{5,21},{6,22},{7,23},{8,24},{9,... | collective-permute-start | bytes 86024 | tf_op jit(solution)/shard_map/ppermute | solution.py:739
  42.3 0.7 concatenate.41
  43.0 0.3 collective-permute-done.5
  43.3 0.1 concatenate.43
  43.4 3.1 %collective-permute-start.6 = (f32[1,112,128]{2,1,0:T(8,128)S(1)}, f32[1,112,128]{2,1,0:T(8,128)S(1)}, u32[]{:S(2)}, u32[]{:S(2)}) collective-permute-start(f32[1,112,128]{2,1,0:T(8,128)S(1)} %add_bitcast_fusion), channel_id=1, source_target_pairs={{0,96},{1,33},{2,98},{3,35},{4,100},{5,37},{6,102},{7,39},{8,104},... | collective-permute-start | bytes 172040 | tf_op jit(solution)/shard_map/ppermute | solution.py:731
  46.5 1.6 %collective-permute-done.6 = f32[1,112,128]{2,1,0:T(8,128)S(1)} collective-permute-done((f32[1,112,128]{2,1,0:T(8,128)S(1)}, f32[1,112,128]{2,1,0:T(8,128)S(1)}, u32[]{:S(2)}, u32[]{:S(2)}) %collective-permute-start.6) | collective-permute-done | bytes 57376 | tf_op jit(solution)/shard_map/ppermute | solution.py:731
  48.1 1.4 %collective-permute-start.7 = (f32[2,112,128]{2,1,0:T(8,128)S(1)}, f32[2,112,128]{2,1,0:T(8,128)S(1)}, u32[]{:S(2)}, u32[]{:S(2)}) collective-permute-start(f32[2,112,128]{2,1,0:T(8,128)S(1)} %pad_maximum_fusion.9), channel_id=1, source_target_pairs={{0,18},{1,3},{2,16},{3,1},{4,22},{5,7},{6,20},{7,5},{8,26},{9,11},... | collective-permute-start | bytes 344072 | tf_op jit(solution)/shard_map/ppermute | solution.py:731
  49.5 2.3 %collective-permute-done.7 = f32[2,112,128]{2,1,0:T(8,128)S(1)} collective-permute-done((f32[2,112,128]{2,1,0:T(8,128)S(1)}, f32[2,112,128]{2,1,0:T(8,128)S(1)}, u32[]{:S(2)}, u32[]{:S(2)}) %collective-permute-start.7) | collective-permute-done | bytes 114720 | tf_op jit(solution)/shard_map/ppermute | solution.py:731
  51.9 2.1 %collective-permute-start.8 = (f32[4,112,128]{2,1,0:T(8,128)S(1)}, f32[4,112,128]{2,1,0:T(8,128)S(1)}, u32[]{:S(2)}, u32[]{:S(2)}) collective-permute-start(f32[4,112,128]{2,1,0:T(8,128)S(1)} %pad_maximum_fusion.7), channel_id=1, source_target_pairs={{0,12},{1,5},{2,14},{3,7},{4,8},{5,1},{6,10},{7,3},{8,4},{9,13},{1... | collective-permute-start | bytes 688136 | tf_op jit(solution)/shard_map/ppermute | solution.py:731
  54.0 3.4 %collective-permute-done.8 = f32[4,112,128]{2,1,0:T(8,128)S(1)} collective-permute-done((f32[4,112,128]{2,1,0:T(8,128)S(1)}, f32[4,112,128]{2,1,0:T(8,128)S(1)}, u32[]{:S(2)}, u32[]{:S(2)}) %collective-permute-start.8) | collective-permute-done | bytes 229408 | tf_op jit(solution)/shard_map/ppermute | solution.py:731
  57.5 1.9 %collective-permute-start.11 = (f32[8,40,128]{2,1,0:T(8,128)S(1)}, f32[8,40,128]{2,1,0:T(8,128)S(1)}, u32[]{:S(2)}, u32[]{:S(2)}) collective-permute-start(f32[8,40,128]{2,1,0:T(8,128)S(1)} %get-tuple-element.30), channel_id=1, source_target_pairs={{0,2},{1,19},{2,0},{3,17},{4,6},{5,23},{6,4},{7,21},{8,10},{9,27},... | collective-permute-start | bytes 491528 | tf_op jit(solution)/shard_map/ppermute | solution.py:731
  59.3 1.6 %collective-permute-start.9 = (f32[8,40,128]{2,1,0:T(8,128)S(1)}, f32[8,40,128]{2,1,0:T(8,128)S(1)}, u32[]{:S(2)}, u32[]{:S(2)}) collective-permute-start(f32[8,40,128]{2,1,0:T(8,128)S(1)} %get-tuple-element.31), channel_id=1, source_target_pairs={{0,32},{1,97},{2,34},{3,99},{4,36},{5,101},{6,38},{7,103},{8,40},{... | collective-permute-start | bytes 491528 | tf_op jit(solution)/shard_map/ppermute | solution.py:731
  60.9 2.0 %collective-permute-done.11 = f32[8,40,128]{2,1,0:T(8,128)S(1)} collective-permute-done((f32[8,40,128]{2,1,0:T(8,128)S(1)}, f32[8,40,128]{2,1,0:T(8,128)S(1)}, u32[]{:S(2)}, u32[]{:S(2)}) %collective-permute-start.11) | collective-permute-done | bytes 163872 | tf_op jit(solution)/shard_map/ppermute | solution.py:731
  62.9 2.2 %collective-permute-start.12 = (f32[16,40,128]{2,1,0:T(8,128)S(1)}, f32[16,40,128]{2,1,0:T(8,128)S(1)}, u32[]{:S(2)}, u32[]{:S(2)}) collective-permute-start(f32[16,40,128]{2,1,0:T(8,128)S(1)} %pad_maximum_fusion.5), channel_id=1, source_target_pairs={{0,4},{1,13},{2,6},{3,15},{4,0},{5,9},{6,2},{7,11},{8,12},{9,5},{1... | collective-permute-start | bytes 983048 | tf_op jit(solution)/shard_map/ppermute | solution.py:731
  65.1 0.7 collective-permute-start.13
  65.8 0.0 collective-permute-done.9
  65.8 1.9 %collective-permute-start.10 = (f32[16,40,128]{2,1,0:T(8,128)S(1)}, f32[16,40,128]{2,1,0:T(8,128)S(1)}, u32[]{:S(2)}, u32[]{:S(2)}) collective-permute-start(f32[16,40,128]{2,1,0:T(8,128)S(1)} %pad_maximum_fusion.4), channel_id=1, source_target_pairs={{0,2},{1,19},{2,0},{3,17},{4,6},{5,23},{6,4},{7,21},{8,10},{9,27},... | collective-permute-start | bytes 983048 | tf_op jit(solution)/shard_map/ppermute | solution.py:731
  67.7 4.5 %collective-permute-done.13 = f32[8,32,128]{2,1,0:T(8,128)S(1)} collective-permute-done((f32[8,32,128]{2,1,0:T(8,128)S(1)}, f32[8,32,128]{2,1,0:T(8,128)S(1)}, u32[]{:S(2)}, u32[]{:S(2)}) %collective-permute-start.13) | collective-permute-done | bytes 131104 | tf_op jit(solution)/shard_map/ppermute | solution.py:731
  72.2 3.0 %collective-permute-start.14 = (f32[16,32,128]{2,1,0:T(8,128)S(1)}, f32[16,32,128]{2,1,0:T(8,128)S(1)}, u32[]{:S(2)}, u32[]{:S(2)}) collective-permute-start(f32[16,32,128]{2,1,0:T(8,128)S(1)} %pad_maximum_fusion.6), channel_id=1, source_target_pairs={{0,32},{1,97},{2,34},{3,99},{4,36},{5,101},{6,38},{7,103},{8,40},{... | collective-permute-start | bytes 786440 | tf_op jit(solution)/shard_map/ppermute | solution.py:731
  75.3 0.1 collective-permute-start.19
  75.5 3.0 %collective-permute-start.18 = (f32[32,40,128]{2,1,0:T(8,128)S(1)}, f32[32,40,128]{2,1,0:T(8,128)S(1)}, u32[]{:S(2)}, u32[]{:S(2)}) collective-permute-start(f32[32,40,128]{2,1,0:T(8,128)S(1)} %pad_maximum_fusion.refs_1_), channel_id=1, source_target_pairs={{0,4},{1,13},{2,6},{3,15},{4,0},{5,9},{6,2},{7,11},{8,12},{9,5},{1... | collective-permute-start | bytes 1966088 | tf_op jit(solution)/shard_map/ppermute | solution.py:731
  78.5 0.5 collective-permute-done.14
  79.1 10.6 %collective-permute-start.17 = (f32[32,32,128]{2,1,0:T(8,128)S(1)}, f32[32,32,128]{2,1,0:T(8,128)S(1)}, u32[]{:S(2)}, u32[]{:S(2)}) collective-permute-start(f32[32,32,128]{2,1,0:T(8,128)S(1)} %pad_maximum_fusion.2.refs_3_), channel_id=1, source_target_pairs={{0,1},{1,0},{2,3},{3,2},{4,5},{5,4},{6,7},{7,6},{8,9},{9,8},{10,11... | collective-permute-start | bytes 1572872 | tf_op jit(solution)/shard_map/ppermute | solution.py:731
  89.7 0.2 collective-permute-start.16
  89.9 1.4 %collective-permute-done.17.refs_6_ = f32[32,32,128]{2,1,0:T(8,128)S(1)} collective-permute-done((f32[32,32,128]{2,1,0:T(8,128)S(1)}, f32[32,32,128]{2,1,0:T(8,128)S(1)}, u32[]{:S(2)}, u32[]{:S(2)}) %collective-permute-start.17) | collective-permute-done | bytes 524320 | tf_op jit(solution)/shard_map/ppermute | solution.py:731
  91.2 0.4 collective-permute-start.15
  91.6 5.0 %collective-permute-start.22 = (f32[32,40,128]{2,1,0:T(8,128)S(1)}, f32[32,40,128]{2,1,0:T(8,128)S(1)}, u32[]{:S(2)}, u32[]{:S(2)}) collective-permute-start(f32[32,40,128]{2,1,0:T(8,128)S(1)} %collective-permute-done.19.refs_3_), channel_id=1, source_target_pairs={{0,1},{1,0},{2,3},{3,2},{4,5},{5,4},{6,7},{7,6},{8,9},{9,8},{10,11... | collective-permute-start | bytes 1966088 | tf_op jit(solution)/shard_map/ppermute | solution.py:731
  96.6 0.0 collective-permute-start.21
  96.6 2.3 %collective-permute-done.20.refs_4_ = f32[32,32,128]{2,1,0:T(8,128)S(1)} collective-permute-done((f32[32,32,128]{2,1,0:T(8,128)S(1)}, f32[32,32,128]{2,1,0:T(8,128)S(1)}, u32[]{:S(2)}, u32[]{:S(2)}) %collective-permute-start.20) | collective-permute-done | bytes 524320 | tf_op jit(solution)/shard_map/ppermute | solution.py:731
  98.9 0.0 collective-permute-start.23
  99.0 2.6 %shard_map.77.refs_1_ = f32[15232,128]{1,0:T(8,128)S(1)} custom-call(s32[2]{0:T(128)S(1)} %pad_add_fusion.place.refs_0_, f32[32,40,128]{2,1,0:T(8,128)S(1)} %pad_maximum_fusion.refs_1_, f32[32,40,128]{2,1,0:T(8,128)S(1)} %pad_maximum_fusion.1.refs_2_, f32[32,32,128]{2,1,0:T(8,128)S(1)} %pad_maximum_fusion.2.refs_3_, ...), custom_call_target="tpu_custom_call" | custom-call | tf_op jit(solution)/shard_map/pallas_call | solution.py:504
  101.5 1.6 %shard_map.78.refs_2_ = f32[15232,128]{1,0:T(8,128)S(1)} custom-call(s32[2]{0:T(128)S(1)} %pad_add_fusion.place.refs_0_, f32[15232,128]{1,0:T(8,128)S(1)} %shard_map.77.refs_1_, f32[32,40,128]{2,1,0:T(8,128)S(1)} %collective-permute-done.18.refs_2_, f32[32,40,128]{2,1,0:T(8,128)S(1)} %collective-permute-done.19.refs_3_, ...), custom_call_target="tpu_custom_call", output_to_operand_aliasing={{}: (1, {})} | custom-call | tf_op jit(solution)/shard_map/pallas_call | solution.py:504
  103.2 17.5 %solve_part.1 = (f32[3,1,2,128]{3,2,1,0:T(2,128)}, f32[15232,128]{1,0:T(8,128)S(1)}) custom-call(s32[2]{0:T(128)S(1)} %pad_add_fusion.place.refs_0_, f32[3,1,2,128]{3,2,1,0:T(2,128)S(1)} %get-tuple-element.16.nodes.refs_1_, f32[15232,128]{1,0:T(8,128)S(1)} %shard_map.78.refs_2_, ...), custom_call_target="tpu_custom_call", output_to_operand_aliasing={{1}: (2, {})} | custom-call | tf_op jit(solution)/shard_map/solve_part/pallas_call | solution.py:690
  (33 shorter events, 0.4 us)
Async XLA Ops:
  2.6 4.7 %collective-permute-start = (f32[32,1024]{1,0:T(8,128)S(1)}, f32[32,1024]{1,0:T(8,128)S(1)}, u32[]{:S(2)}, u32[]{:S(2)}) collective-permute-start(f32[32,1024]{1,0:T(8,128)S(1)} %get-tuple-element.18), channel_id=1, source_target_pairs={{0,1},{1,0},{2,3},{3,2},{4,5},{5,4},{6,7},{7,6},{8,9},{9,8},{10,11... | collective-permute-start | bytes 393224 | tf_op jit(solution)/shard_map/ppermute | solution.py:749
  4.0 7.2 %collective-permute-start.1 = (f32[32,1024]{1,0:T(8,128)S(1)}, f32[32,1024]{1,0:T(8,128)S(1)}, u32[]{:S(2)}, u32[]{:S(2)}) collective-permute-start(f32[32,1024]{1,0:T(8,128)S(1)} %get-tuple-element.19), channel_id=1, source_target_pairs={{1,2},{2,1},{3,4},{4,3},{5,6},{6,5},{7,8},{8,7},{9,10},{10,9},{11,... | collective-permute-start | bytes 393224 | tf_op jit(solution)/shard_map/ppermute | solution.py:749
  11.8 6.6 %collective-permute-start.2 = (f32[56,1024]{1,0:T(8,128)S(1)}, f32[56,1024]{1,0:T(8,128)S(1)}, u32[]{:S(2)}, u32[]{:S(2)}) collective-permute-start(f32[56,1024]{1,0:T(8,128)S(1)} %get-tuple-element.23), channel_id=1, source_target_pairs={{0,16},{16,0},{32,48},{48,32},{64,80},{80,64},{96,112},{112,96},{1... | collective-permute-start | bytes 688136 | tf_op jit(solution)/shard_map/ppermute | solution.py:749
  15.0 3.4 %collective-permute-start.3 = (f32[56,1024]{1,0:T(8,128)S(1)}, f32[56,1024]{1,0:T(8,128)S(1)}, u32[]{:S(2)}, u32[]{:S(2)}) collective-permute-start(f32[56,1024]{1,0:T(8,128)S(1)} %get-tuple-element.24), channel_id=1, source_target_pairs={{16,32},{32,16},{48,64},{64,48},{80,96},{96,80},{17,33},{33,17},{4... | collective-permute-start | bytes 688136 | tf_op jit(solution)/shard_map/ppermute | solution.py:749
  24.6 11.1 %collective-permute-start.4 = (f32[48,128]{1,0:T(8,128)S(1)}, f32[48,128]{1,0:T(8,128)S(1)}, u32[]{:S(2)}, u32[]{:S(2)}) collective-permute-start(f32[48,128]{1,0:T(8,128)S(1)} %get-tuple-element.26), channel_id=1, source_target_pairs={{0,1},{1,2},{2,3},{3,4},{4,5},{5,6},{6,7},{7,8},{8,9},{9,10},{10,1... | collective-permute-start | bytes 73736 | tf_op jit(solution)/shard_map/ppermute | solution.py:739
  36.1 7.2 %collective-permute-start.5 = (f32[56,128]{1,0:T(8,128)S(1)}, f32[56,128]{1,0:T(8,128)S(1)}, u32[]{:S(2)}, u32[]{:S(2)}) collective-permute-start(f32[56,128]{1,0:T(8,128)S(1)} %add.10), channel_id=1, source_target_pairs={{0,16},{1,17},{2,18},{3,19},{4,20},{5,21},{6,22},{7,23},{8,24},{9,... | collective-permute-start | bytes 86024 | tf_op jit(solution)/shard_map/ppermute | solution.py:739
  43.4 4.7 %collective-permute-start.6 = (f32[1,112,128]{2,1,0:T(8,128)S(1)}, f32[1,112,128]{2,1,0:T(8,128)S(1)}, u32[]{:S(2)}, u32[]{:S(2)}) collective-permute-start(f32[1,112,128]{2,1,0:T(8,128)S(1)} %add_bitcast_fusion), channel_id=1, source_target_pairs={{0,96},{1,33},{2,98},{3,35},{4,100},{5,37},{6,102},{7,39},{8,104},... | collective-permute-start | bytes 172040 | tf_op jit(solution)/shard_map/ppermute | solution.py:731
  48.1 3.7 %collective-permute-start.7 = (f32[2,112,128]{2,1,0:T(8,128)S(1)}, f32[2,112,128]{2,1,0:T(8,128)S(1)}, u32[]{:S(2)}, u32[]{:S(2)}) collective-permute-start(f32[2,112,128]{2,1,0:T(8,128)S(1)} %pad_maximum_fusion.9), channel_id=1, source_target_pairs={{0,18},{1,3},{2,16},{3,1},{4,22},{5,7},{6,20},{7,5},{8,26},{9,11},... | collective-permute-start | bytes 344072 | tf_op jit(solution)/shard_map/ppermute | solution.py:731
  51.9 5.5 %collective-permute-start.8 = (f32[4,112,128]{2,1,0:T(8,128)S(1)}, f32[4,112,128]{2,1,0:T(8,128)S(1)}, u32[]{:S(2)}, u32[]{:S(2)}) collective-permute-start(f32[4,112,128]{2,1,0:T(8,128)S(1)} %pad_maximum_fusion.7), channel_id=1, source_target_pairs={{0,12},{1,5},{2,14},{3,7},{4,8},{5,1},{6,10},{7,3},{8,4},{9,13},{1... | collective-permute-start | bytes 688136 | tf_op jit(solution)/shard_map/ppermute | solution.py:731
  57.5 5.5 %collective-permute-start.11 = (f32[8,40,128]{2,1,0:T(8,128)S(1)}, f32[8,40,128]{2,1,0:T(8,128)S(1)}, u32[]{:S(2)}, u32[]{:S(2)}) collective-permute-start(f32[8,40,128]{2,1,0:T(8,128)S(1)} %get-tuple-element.30), channel_id=1, source_target_pairs={{0,2},{1,19},{2,0},{3,17},{4,6},{5,23},{6,4},{7,21},{8,10},{9,27},... | collective-permute-start | bytes 491528 | tf_op jit(solution)/shard_map/ppermute | solution.py:731
  59.3 6.5 %collective-permute-start.9 = (f32[8,40,128]{2,1,0:T(8,128)S(1)}, f32[8,40,128]{2,1,0:T(8,128)S(1)}, u32[]{:S(2)}, u32[]{:S(2)}) collective-permute-start(f32[8,40,128]{2,1,0:T(8,128)S(1)} %get-tuple-element.31), channel_id=1, source_target_pairs={{0,32},{1,97},{2,34},{3,99},{4,36},{5,101},{6,38},{7,103},{8,40},{... | collective-permute-start | bytes 491528 | tf_op jit(solution)/shard_map/ppermute | solution.py:731
  62.9 12.3 %collective-permute-start.12 = (f32[16,40,128]{2,1,0:T(8,128)S(1)}, f32[16,40,128]{2,1,0:T(8,128)S(1)}, u32[]{:S(2)}, u32[]{:S(2)}) collective-permute-start(f32[16,40,128]{2,1,0:T(8,128)S(1)} %pad_maximum_fusion.5), channel_id=1, source_target_pairs={{0,4},{1,13},{2,6},{3,15},{4,0},{5,9},{6,2},{7,11},{8,12},{9,5},{1... | collective-permute-start | bytes 983048 | tf_op jit(solution)/shard_map/ppermute | solution.py:731
  65.1 7.1 %collective-permute-start.13 = (f32[8,32,128]{2,1,0:T(8,128)S(1)}, f32[8,32,128]{2,1,0:T(8,128)S(1)}, u32[]{:S(2)}, u32[]{:S(2)}) collective-permute-start(f32[8,32,128]{2,1,0:T(8,128)S(1)} %pad_maximum_fusion.8), channel_id=1, source_target_pairs={{0,4},{1,13},{2,6},{3,15},{4,0},{5,9},{6,2},{7,11},{8,12},{9,5},{1... | collective-permute-start | bytes 393224 | tf_op jit(solution)/shard_map/ppermute | solution.py:731
  65.8 9.6 %collective-permute-start.10 = (f32[16,40,128]{2,1,0:T(8,128)S(1)}, f32[16,40,128]{2,1,0:T(8,128)S(1)}, u32[]{:S(2)}, u32[]{:S(2)}) collective-permute-start(f32[16,40,128]{2,1,0:T(8,128)S(1)} %pad_maximum_fusion.4), channel_id=1, source_target_pairs={{0,2},{1,19},{2,0},{3,17},{4,6},{5,23},{6,4},{7,21},{8,10},{9,27},... | collective-permute-start | bytes 983048 | tf_op jit(solution)/shard_map/ppermute | solution.py:731
  72.2 6.8 %collective-permute-start.14 = (f32[16,32,128]{2,1,0:T(8,128)S(1)}, f32[16,32,128]{2,1,0:T(8,128)S(1)}, u32[]{:S(2)}, u32[]{:S(2)}) collective-permute-start(f32[16,32,128]{2,1,0:T(8,128)S(1)} %pad_maximum_fusion.6), channel_id=1, source_target_pairs={{0,32},{1,97},{2,34},{3,99},{4,36},{5,101},{6,38},{7,103},{8,40},{... | collective-permute-start | bytes 786440 | tf_op jit(solution)/shard_map/ppermute | solution.py:731
  75.3 16.3 %collective-permute-start.19 = (f32[32,40,128]{2,1,0:T(8,128)S(1)}, f32[32,40,128]{2,1,0:T(8,128)S(1)}, u32[]{:S(2)}, u32[]{:S(2)}) collective-permute-start(f32[32,40,128]{2,1,0:T(8,128)S(1)} %pad_maximum_fusion.1.refs_2_), channel_id=1, source_target_pairs={{0,32},{1,97},{2,34},{3,99},{4,36},{5,101},{6,38},{7,103},{8,40},{... | collective-permute-start | bytes 1966088 | tf_op jit(solution)/shard_map/ppermute | solution.py:731
  75.5 21.1 %collective-permute-start.18 = (f32[32,40,128]{2,1,0:T(8,128)S(1)}, f32[32,40,128]{2,1,0:T(8,128)S(1)}, u32[]{:S(2)}, u32[]{:S(2)}) collective-permute-start(f32[32,40,128]{2,1,0:T(8,128)S(1)} %pad_maximum_fusion.refs_1_), channel_id=1, source_target_pairs={{0,4},{1,13},{2,6},{3,15},{4,0},{5,9},{6,2},{7,11},{8,12},{9,5},{1... | collective-permute-start | bytes 1966088 | tf_op jit(solution)/shard_map/ppermute | solution.py:731
  79.1 12.1 %collective-permute-start.17 = (f32[32,32,128]{2,1,0:T(8,128)S(1)}, f32[32,32,128]{2,1,0:T(8,128)S(1)}, u32[]{:S(2)}, u32[]{:S(2)}) collective-permute-start(f32[32,32,128]{2,1,0:T(8,128)S(1)} %pad_maximum_fusion.2.refs_3_), channel_id=1, source_target_pairs={{0,1},{1,0},{2,3},{3,2},{4,5},{5,4},{6,7},{7,6},{8,9},{9,8},{10,11... | collective-permute-start | bytes 1572872 | tf_op jit(solution)/shard_map/ppermute | solution.py:731
  89.7 9.2 %collective-permute-start.20 = (f32[32,32,128]{2,1,0:T(8,128)S(1)}, f32[32,32,128]{2,1,0:T(8,128)S(1)}, u32[]{:S(2)}, u32[]{:S(2)}) collective-permute-start(f32[32,32,128]{2,1,0:T(8,128)S(1)} %pad_maximum_fusion.2.refs_3_), channel_id=1, source_target_pairs={{0,2},{1,19},{2,0},{3,17},{4,6},{5,23},{6,4},{7,21},{8,10},{9,27},... | collective-permute-start | bytes 1572872 | tf_op jit(solution)/shard_map/ppermute | solution.py:731
  89.7 9.3 %collective-permute-start.16 = (f32[32,40,128]{2,1,0:T(8,128)S(1)}, f32[32,40,128]{2,1,0:T(8,128)S(1)}, u32[]{:S(2)}, u32[]{:S(2)}) collective-permute-start(f32[32,40,128]{2,1,0:T(8,128)S(1)} %pad_maximum_fusion.1.refs_2_), channel_id=1, source_target_pairs={{0,1},{1,0},{2,3},{3,2},{4,5},{5,4},{6,7},{7,6},{8,9},{9,8},{10,11... | collective-permute-start | bytes 1966088 | tf_op jit(solution)/shard_map/ppermute | solution.py:731
  91.2 7.7 %collective-permute-start.15 = (f32[32,40,128]{2,1,0:T(8,128)S(1)}, f32[32,40,128]{2,1,0:T(8,128)S(1)}, u32[]{:S(2)}, u32[]{:S(2)}) collective-permute-start(f32[32,40,128]{2,1,0:T(8,128)S(1)} %pad_maximum_fusion.refs_1_), channel_id=1, source_target_pairs={{0,1},{1,0},{2,3},{3,2},{4,5},{5,4},{6,7},{7,6},{8,9},{9,8},{10,11... | collective-permute-start | bytes 1966088 | tf_op jit(solution)/shard_map/ppermute | solution.py:731
  91.6 11.6 %collective-permute-start.22 = (f32[32,40,128]{2,1,0:T(8,128)S(1)}, f32[32,40,128]{2,1,0:T(8,128)S(1)}, u32[]{:S(2)}, u32[]{:S(2)}) collective-permute-start(f32[32,40,128]{2,1,0:T(8,128)S(1)} %collective-permute-done.19.refs_3_), channel_id=1, source_target_pairs={{0,1},{1,0},{2,3},{3,2},{4,5},{5,4},{6,7},{7,6},{8,9},{9,8},{10,11... | collective-permute-start | bytes 1966088 | tf_op jit(solution)/shard_map/ppermute | solution.py:731
  96.6 6.6 %collective-permute-start.21 = (f32[32,40,128]{2,1,0:T(8,128)S(1)}, f32[32,40,128]{2,1,0:T(8,128)S(1)}, u32[]{:S(2)}, u32[]{:S(2)}) collective-permute-start(f32[32,40,128]{2,1,0:T(8,128)S(1)} %collective-permute-done.18.refs_2_), channel_id=1, source_target_pairs={{0,1},{1,0},{2,3},{3,2},{4,5},{5,4},{6,7},{7,6},{8,9},{9,8},{10,11... | collective-permute-start | bytes 1966088 | tf_op jit(solution)/shard_map/ppermute | solution.py:731
  98.9 4.2 %collective-permute-start.23 = (f32[32,32,128]{2,1,0:T(8,128)S(1)}, f32[32,32,128]{2,1,0:T(8,128)S(1)}, u32[]{:S(2)}, u32[]{:S(2)}) collective-permute-start(f32[32,32,128]{2,1,0:T(8,128)S(1)} %collective-permute-done.20.refs_4_), channel_id=1, source_target_pairs={{0,1},{1,0},{2,3},{3,2},{4,5},{5,4},{6,7},{7,6},{8,9},{9,8},{10,11... | collective-permute-start | bytes 1572872 | tf_op jit(solution)/shard_map/ppermute | solution.py:731
